TPU v7x, 32 devices: a whole 2x2x4 slice. The times are simulated.
32 devices in a mesh: section: 4 (over z), space: 8 (over y, x, core).
Axes of the slice: x: 2, y: 2, z: 4, core: 2. Of those that a mesh axis runs over, the one named last changes fastest.
Arguments:
- act_in: bfloat16 [4, 4096, 512], P('section', 'space'), may hold values from -6 to 6
- stash: bfloat16 [4, 4, 4096, 512], P('section', None, 'space'), may hold values from -6 to 6
- plan: int32 [4], P('section'), may hold values from 0 to 3
- grad_in: bfloat16 [4, 4096, 512], P('section', 'space'), may hold values from -6 to 6
- fwd_owner: int32 [4, 4096], P('section', 'space'), may hold values from 0 to 7, as said below
- stash_owner: int32 [4, 4, 4096], P('section', None, 'space'), may hold values from 0 to 7, as said below
- ln_gain: float32 [4, 512], P('section'), may hold values from 0.5 to 1.5
- qkv_weight: bfloat16 [4, 512, 1536], P('section')
- proj_weight: bfloat16 [4, 512, 512], P('section'), may hold values from -1 to 1
Outputs:
- act_out: bfloat16 [4, 4096, 512], P('section', 'space')
- grad_out: bfloat16 [4, 4096, 512], P('section', 'space')
Inputs may be any that keep to these rules, and one draw needn't show every extreme that they name: `fwd_owner`: within each group of 512 rows of one list, owners never decrease; each group sends 128 rows to a quarter of the owners, 64 rows to half of them and none to the rest; in each list one owner gets 128 rows from every group. `stash_owner`: same law for each section and stored microbatch, independently drawn.
All inputs are finite; a program needn't handle non-finite values.
Results may differ from a plain program's by a relative error of at most 0.004.
The roundings to bfloat16 on the way count: a program that leaves them out, or rounds other values in their place, can miss the bound.
Values may be sent and summed in bfloat16 or wider, within the bound.
A program may use at most 128 MiB of HBM per device.

v0:
```python
import math

import jax
import jax.numpy as jnp
from jax import lax
from jax.sharding import PartitionSpec as P

HEADS = 32


EPS = 1e-05
NEG = -1e30
HEAD_GROUP = 2


def passed_along(value, axis, by):
    size = lax.axis_size(axis)
    pairs = [(i, i + by) for i in range(size) if 0 <= i + by < size]
    return lax.ppermute(value, axis, pairs)


def normalize(rows_in, gain):
    values = rows_in.astype(jnp.float32)
    center = values - jnp.mean(values, axis=-1, keepdims=True)
    spread = jnp.mean(center * center, axis=-1, keepdims=True)
    return center * lax.rsqrt(spread + EPS) * gain


def split_heads(block, head_dim):
    return block.reshape(block.shape[0], block.shape[1] // head_dim, head_dim)


def block_probs(query, key_rows, live, scale):
    score = jnp.einsum("qhd,khd->hqk", query, key_rows, preferred_element_type=jnp.float32) * scale
    score = jnp.where(live[None, None, :], score, NEG)
    top = jnp.max(score, axis=2, keepdims=True)
    expd = jnp.exp(score - top)
    return expd / jnp.sum(expd, axis=2, keepdims=True)


def attend(patch, live, heads):
    width = patch.shape[1] // 3
    head_dim = width // heads
    span = HEAD_GROUP * head_dim
    scale = 1.0 / math.sqrt(head_dim)
    slots = patch.shape[0]

    def one_block(block_index, totals):
        start = block_index * span
        query = split_heads(lax.dynamic_slice_in_dim(patch, start, span, 1), head_dim)
        key_rows = split_heads(lax.dynamic_slice_in_dim(patch, width + start, span, 1), head_dim)
        value_rows = split_heads(
            lax.dynamic_slice_in_dim(patch, 2 * width + start, span, 1), head_dim
        )
        probs = block_probs(query, key_rows, live, scale).astype(jnp.bfloat16)
        result = jnp.einsum(
            "hqk,khd->qhd", probs, value_rows, preferred_element_type=jnp.float32
        ).reshape(slots, span)
        return lax.dynamic_update_slice_in_dim(totals, result, start, 1)

    return lax.fori_loop(0, heads // HEAD_GROUP, one_block, jnp.zeros((slots, width), jnp.float32))


def attend_grad(patch, live, upstream, heads):
    width = patch.shape[1] // 3
    head_dim = width // heads
    span = HEAD_GROUP * head_dim
    scale = 1.0 / math.sqrt(head_dim)
    slots = patch.shape[0]

    def one_block(block_index, totals):
        start = block_index * span
        query = split_heads(lax.dynamic_slice_in_dim(patch, start, span, 1), head_dim)
        key_rows = split_heads(lax.dynamic_slice_in_dim(patch, width + start, span, 1), head_dim)
        value_rows = split_heads(
            lax.dynamic_slice_in_dim(patch, 2 * width + start, span, 1), head_dim
        )
        out_grad = split_heads(lax.dynamic_slice_in_dim(upstream, start, span, 1), head_dim)
        probs = block_probs(query, key_rows, live, scale)
        rounded = probs.astype(jnp.bfloat16)
        prob_grad = jnp.einsum(
            "qhd,khd->hqk", out_grad, value_rows, preferred_element_type=jnp.float32
        )
        value_grad = jnp.einsum(
            "hqk,qhd->khd", rounded, out_grad, preferred_element_type=jnp.float32
        ).reshape(slots, span)
        delta = jnp.sum(prob_grad * probs, axis=2, keepdims=True)
        score_grad = (probs * (prob_grad - delta) * scale).astype(jnp.bfloat16)
        query_grad = jnp.einsum(
            "hqk,khd->qhd", score_grad, key_rows, preferred_element_type=jnp.float32
        ).reshape(slots, span)
        key_grad = jnp.einsum(
            "hqk,qhd->khd", score_grad, query, preferred_element_type=jnp.float32
        ).reshape(slots, span)
        totals = lax.dynamic_update_slice_in_dim(totals, query_grad, start, 1)
        totals = lax.dynamic_update_slice_in_dim(totals, key_grad, width + start, 1)
        return lax.dynamic_update_slice_in_dim(totals, value_grad, 2 * width + start, 1)

    return lax.fori_loop(
        0, heads // HEAD_GROUP, one_block, jnp.zeros((slots, 3 * width), jnp.float32)
    )


def layout(owners, groups, cap):
    rows = owners.shape[0]
    labels = jnp.arange(groups, dtype=jnp.int32)
    onehot = (owners[:, None] == labels[None, :]).astype(jnp.int32)
    counts = jnp.sum(onehot, axis=0)
    offsets = jnp.cumsum(counts) - counts
    slots = jnp.arange(cap, dtype=jnp.int32)
    valid = slots[None, :] < counts[:, None]
    index = jnp.where(valid, offsets[:, None] + slots[None, :], 0)
    rank = jnp.arange(rows, dtype=jnp.int32) - jnp.sum(onehot * offsets[None, :], axis=1)
    back = owners * cap + rank
    return (index, valid, back)


def pack_rows(source, index, valid):
    picked = jnp.take(source, index.reshape(-1), axis=0).reshape(index.shape + (source.shape[1],))
    return jnp.where(valid[..., None], picked, jnp.zeros((), source.dtype))


def project(rows_in, w_qkv):
    return jnp.dot(rows_in, w_qkv, preferred_element_type=jnp.float32).astype(jnp.bfloat16)


def on_device(
    act_in, stash, plan, grad_in, fwd_owner, stash_owner, ln_gain, qkv_weight, proj_weight
):
    groups = lax.axis_size("space")
    rows_in = act_in[0]
    rows = rows_in.shape[0]
    width = rows_in.shape[1]
    cap = 2 * rows // groups
    slots_all = groups * cap
    gain = ln_gain[0]
    w_qkv = qkv_weight[0]
    w_proj = proj_weight[0]
    pick = plan[0]
    stored = lax.dynamic_index_in_dim(stash[0], pick, 0, keepdims=False)
    stored_owners = lax.dynamic_index_in_dim(stash_owner[0], pick, 0, keepdims=False)
    upstream = grad_in[0]
    normed = normalize(rows_in, gain).astype(jnp.bfloat16)
    normed_b = normalize(stored, gain).astype(jnp.bfloat16)
    out_grad = jnp.dot(upstream, w_proj.T, preferred_element_type=jnp.float32).astype(jnp.bfloat16)
    payload = project(normed, w_qkv)
    payload_b = project(normed_b, w_qkv)
    index, valid, back = layout(fwd_owner[0], groups, cap)
    index_b, valid_b, back_b = layout(stored_owners, groups, cap)
    send_rows = pack_rows(payload, index, valid)
    send_flags = valid.astype(jnp.bfloat16)
    send_rows_b = pack_rows(payload_b, index_b, valid_b)
    send_flags_b = valid_b.astype(jnp.bfloat16)
    send_grads = pack_rows(out_grad, index_b, valid_b)
    got_rows, got_flags = (
        lax.all_to_all(send_rows, "space", split_axis=0, concat_axis=0, tiled=True),
        lax.all_to_all(send_flags, "space", split_axis=0, concat_axis=0, tiled=True),
    )
    got_rows_b, got_flags_b = (
        lax.all_to_all(send_rows_b, "space", split_axis=0, concat_axis=0, tiled=True),
        lax.all_to_all(send_flags_b, "space", split_axis=0, concat_axis=0, tiled=True),
    )
    got_grads = lax.all_to_all(send_grads, "space", split_axis=0, concat_axis=0, tiled=True)
    patch = got_rows.reshape(slots_all, got_rows.shape[-1])
    patch_b = got_rows_b.reshape(slots_all, got_rows_b.shape[-1])
    live = got_flags.reshape(slots_all) > 0.5
    live_b = got_flags_b.reshape(slots_all) > 0.5
    attended = attend(patch, live, HEADS).astype(jnp.bfloat16).reshape(groups, cap, width)
    qkv_grads = attend_grad(patch_b, live_b, got_grads.reshape(slots_all, width), HEADS).astype(
        jnp.bfloat16
    )
    slot_qkv = qkv_grads.reshape(groups, cap, 3 * width)
    ret_att = lax.all_to_all(attended, "space", split_axis=0, concat_axis=0, tiled=True)
    ret_grads = lax.all_to_all(slot_qkv, "space", split_axis=0, concat_axis=0, tiled=True)
    grad_rows = jnp.take(ret_grads.reshape(slots_all, 3 * width), back_b, axis=0)
    normed_grad = jnp.dot(grad_rows, w_qkv.T, preferred_element_type=jnp.float32)
    att_rows = jnp.take(ret_att.reshape(slots_all, width), back, axis=0)
    mixed = (
        rows_in.astype(jnp.float32) + jnp.dot(att_rows, w_proj, preferred_element_type=jnp.float32)
    ).astype(jnp.bfloat16)
    unused, pull = jax.vjp(lambda values: normalize(values, gain), stored.astype(jnp.float32))
    input_grad = (upstream.astype(jnp.float32) + pull(normed_grad)[0]).astype(jnp.bfloat16)
    act_out = passed_along(mixed[None], "section", 1)
    grad_out = passed_along(input_grad[None], "section", -1)
    return (act_out, grad_out)


def solution(mesh):
    in_specs = (
        P("section", "space", None),
        P("section", None, "space", None),
        P("section"),
        P("section", "space", None),
        P("section", "space"),
        P("section", None, "space"),
        P("section", None),
        P("section", None, None),
        P("section", None, None),
    )
    out_specs = (P("section", "space", None), P("section", "space", None))
    return jax.shard_map(
        on_device, mesh=mesh, in_specs=in_specs, out_specs=out_specs, check_vma=False
    )
```

profile of v0, /device:TPU:10, one launch (start us, length us, event | category | flops | bytes accessed | tf_op | source)
XLA Modules:
  0.0 1101.2 jit_solution(14951067177431255770)
XLA Ops:
  44.7 9.5 all-to-all-done.5
  72.7 23.9 %all-to-all-done.3 = bf16[8,128,1536]{2,1,0:T(8,128)(2,1)} async-done(((bf16[8,128,1536]{2,1,0:T(8,128)(2,1)}), bf16[8,128,1536]{2,1,0:T(8,128)(2,1)}, u32[]{:S(2)}, u32[]{:S(2)}) %all-to-all-start.3) | async-done | bytes 3145760 | tf_op jit(solution)/shard_map/all_to_all | solution.py:160
  107.6 31.3 %all-to-all-done = bf16[8,128,1536]{2,1,0:T(8,128)(2,1)} async-done(((bf16[8,128,1536]{2,1,0:T(8,128)(2,1)}), bf16[8,128,1536]{2,1,0:T(8,128)(2,1)}, u32[]{:S(2)}, u32[]{:S(2)}) %all-to-all-start) | async-done | bytes 3145760 | tf_op jit(solution)/shard_map/all_to_all | solution.py:156
  143.7 179.0 %while.30 = (s32[]{:T(128)}, bf16[1024,512]{0,1:T(8,128)(2,1)S(1)}, bf16[1024,1536]{0,1:T(8,128)(2,1)}, pred[1024]{0:T(1024)(128)(4,1)S(1)}, s32[]{:T(128)}, /*i...) while((s32[]{:T(128)}, bf16[1024,512]{0,1:T(8,128)(2,1)S(1)}, ...), condition=%wide.region_8.10_spmd, body=%wide.region_5.9_spmd.sunk | while | flops 146801680 | bytes 17581340 | solution.py:61
  144.7 6.2 fusion.130
  155.9 6.2 fusion.130
  178.2 6.2 fusion.130
  189.4 6.2 fusion.130
  211.8 6.2 fusion.130
  245.4 6.2 fusion.130
  256.6 6.2 fusion.130
  331.8 695.5 %while.31 = (s32[]{:T(128)}, bf16[1024,1536]{0,1:T(8,128)(2,1)}, bf16[1024,1536]{0,1:T(8,128)(2,1)}, pred[1024]{0:T(1024)(128)(4,1)S(1)}, bf16[1024,512]{0,1:T(8...) while((s32[]{:T(128)}, bf16[1024,1536]{0,1:T(8,128)(2,1)}, ...), condition=%wide.region_18.20_spmd, body=%wide.region_14.19_spmd.sunk | while | flops 377494528 | bytes 60327216 | solution.py:99
  343.4 12.1 %fusion.145 = bf16[2,16,1024]{2,1,0:T(8,128)(2,1)S(1)} fusion(bf16[1024,2,16]{0,2,1:T(8,128)(2,1)S(1)} %bitcast.217, f32[2,1024,1024]{1,2,0:T(8,128)} %fusion.142, f32[2,1024,1024]{1,2,0:T(8,128)} %get-tuple-element.366, f32[2,1024]{1,0:T(2,128)S(1)} %get-tuple-element.367), kind=kOutput, calls=%fused_computation.35.clone.1 | convolution fusion | flops 81792000 | bytes 16916480 | tf_op jit(solution)/shard_map/while/body/eval_jaxpr/hqk,qhd->khd/dot_general | solution.py:92
  355.5 13.3 %fusion.144 = bf16[2,16,1024]{2,1,0:T(8,128)(2,1)S(1)} fusion(bf16[1024,2,16]{0,2,1:T(8,128)(2,1)S(1)} %bitcast.215, f32[2,1024,1024]{1,2,0:T(8,128)} %fusion.142, f32[2,1024,1024]{1,2,0:T(8,128)} %get-tuple-element.366, f32[2,1024]{1,0:T(2,128)S(1)} %get-tuple-element.367), kind=kOutput, calls=%fused_computation.36.clone.1 | convolution fusion | flops 81792000 | bytes 16916480 | tf_op jit(solution)/shard_map/while/body/eval_jaxpr/hqk,khd->qhd/dot_general | solution.py:89
  386.9 12.1 %fusion.145 = bf16[2,16,1024]{2,1,0:T(8,128)(2,1)S(1)} fusion(bf16[1024,2,16]{0,2,1:T(8,128)(2,1)S(1)} %bitcast.217, f32[2,1024,1024]{1,2,0:T(8,128)} %fusion.142, f32[2,1024,1024]{1,2,0:T(8,128)} %get-tuple-element.366, f32[2,1024]{1,0:T(2,128)S(1)} %get-tuple-element.367), kind=kOutput, calls=%fused_computation.35.clone.1 | convolution fusion | flops 81792000 | bytes 16916480 | tf_op jit(solution)/shard_map/while/body/eval_jaxpr/hqk,qhd->khd/dot_general | solution.py:92
  399.0 13.3 %fusion.144 = bf16[2,16,1024]{2,1,0:T(8,128)(2,1)S(1)} fusion(bf16[1024,2,16]{0,2,1:T(8,128)(2,1)S(1)} %bitcast.215, f32[2,1024,1024]{1,2,0:T(8,128)} %fusion.142, f32[2,1024,1024]{1,2,0:T(8,128)} %get-tuple-element.366, f32[2,1024]{1,0:T(2,128)S(1)} %get-tuple-element.367), kind=kOutput, calls=%fused_computation.36.clone.1 | convolution fusion | flops 81792000 | bytes 16916480 | tf_op jit(solution)/shard_map/while/body/eval_jaxpr/hqk,khd->qhd/dot_general | solution.py:89
  430.3 12.1 %fusion.145 = bf16[2,16,1024]{2,1,0:T(8,128)(2,1)S(1)} fusion(bf16[1024,2,16]{0,2,1:T(8,128)(2,1)S(1)} %bitcast.217, f32[2,1024,1024]{1,2,0:T(8,128)} %fusion.142, f32[2,1024,1024]{1,2,0:T(8,128)} %get-tuple-element.366, f32[2,1024]{1,0:T(2,128)S(1)} %get-tuple-element.367), kind=kOutput, calls=%fused_computation.35.clone.1 | convolution fusion | flops 81792000 | bytes 16916480 | tf_op jit(solution)/shard_map/while/body/eval_jaxpr/hqk,qhd->khd/dot_general | solution.py:92
  442.4 13.3 %fusion.144 = bf16[2,16,1024]{2,1,0:T(8,128)(2,1)S(1)} fusion(bf16[1024,2,16]{0,2,1:T(8,128)(2,1)S(1)} %bitcast.215, f32[2,1024,1024]{1,2,0:T(8,128)} %fusion.142, f32[2,1024,1024]{1,2,0:T(8,128)} %get-tuple-element.366, f32[2,1024]{1,0:T(2,128)S(1)} %get-tuple-element.367), kind=kOutput, calls=%fused_computation.36.clone.1 | convolution fusion | flops 81792000 | bytes 16916480 | tf_op jit(solution)/shard_map/while/body/eval_jaxpr/hqk,khd->qhd/dot_general | solution.py:89
  473.8 12.1 %fusion.145 = bf16[2,16,1024]{2,1,0:T(8,128)(2,1)S(1)} fusion(bf16[1024,2,16]{0,2,1:T(8,128)(2,1)S(1)} %bitcast.217, f32[2,1024,1024]{1,2,0:T(8,128)} %fusion.142, f32[2,1024,1024]{1,2,0:T(8,128)} %get-tuple-element.366, f32[2,1024]{1,0:T(2,128)S(1)} %get-tuple-element.367), kind=kOutput, calls=%fused_computation.35.clone.1 | convolution fusion | flops 81792000 | bytes 16916480 | tf_op jit(solution)/shard_map/while/body/eval_jaxpr/hqk,qhd->khd/dot_general | solution.py:92
  485.9 13.3 %fusion.144 = bf16[2,16,1024]{2,1,0:T(8,128)(2,1)S(1)} fusion(bf16[1024,2,16]{0,2,1:T(8,128)(2,1)S(1)} %bitcast.215, f32[2,1024,1024]{1,2,0:T(8,128)} %fusion.142, f32[2,1024,1024]{1,2,0:T(8,128)} %get-tuple-element.366, f32[2,1024]{1,0:T(2,128)S(1)} %get-tuple-element.367), kind=kOutput, calls=%fused_computation.36.clone.1 | convolution fusion | flops 81792000 | bytes 16916480 | tf_op jit(solution)/shard_map/while/body/eval_jaxpr/hqk,khd->qhd/dot_general | solution.py:89
  517.3 12.1 %fusion.145 = bf16[2,16,1024]{2,1,0:T(8,128)(2,1)S(1)} fusion(bf16[1024,2,16]{0,2,1:T(8,128)(2,1)S(1)} %bitcast.217, f32[2,1024,1024]{1,2,0:T(8,128)} %fusion.142, f32[2,1024,1024]{1,2,0:T(8,128)} %get-tuple-element.366, f32[2,1024]{1,0:T(2,128)S(1)} %get-tuple-element.367), kind=kOutput, calls=%fused_computation.35.clone.1 | convolution fusion | flops 81792000 | bytes 16916480 | tf_op jit(solution)/shard_map/while/body/eval_jaxpr/hqk,qhd->khd/dot_general | solution.py:92
  529.4 13.3 %fusion.144 = bf16[2,16,1024]{2,1,0:T(8,128)(2,1)S(1)} fusion(bf16[1024,2,16]{0,2,1:T(8,128)(2,1)S(1)} %bitcast.215, f32[2,1024,1024]{1,2,0:T(8,128)} %fusion.142, f32[2,1024,1024]{1,2,0:T(8,128)} %get-tuple-element.366, f32[2,1024]{1,0:T(2,128)S(1)} %get-tuple-element.367), kind=kOutput, calls=%fused_computation.36.clone.1 | convolution fusion | flops 81792000 | bytes 16916480 | tf_op jit(solution)/shard_map/while/body/eval_jaxpr/hqk,khd->qhd/dot_general | solution.py:89
  560.7 12.1 %fusion.145 = bf16[2,16,1024]{2,1,0:T(8,128)(2,1)S(1)} fusion(bf16[1024,2,16]{0,2,1:T(8,128)(2,1)S(1)} %bitcast.217, f32[2,1024,1024]{1,2,0:T(8,128)} %fusion.142, f32[2,1024,1024]{1,2,0:T(8,128)} %get-tuple-element.366, f32[2,1024]{1,0:T(2,128)S(1)} %get-tuple-element.367), kind=kOutput, calls=%fused_computation.35.clone.1 | convolution fusion | flops 81792000 | bytes 16916480 | tf_op jit(solution)/shard_map/while/body/eval_jaxpr/hqk,qhd->khd/dot_general | solution.py:92
  572.9 13.3 %fusion.144 = bf16[2,16,1024]{2,1,0:T(8,128)(2,1)S(1)} fusion(bf16[1024,2,16]{0,2,1:T(8,128)(2,1)S(1)} %bitcast.215, f32[2,1024,1024]{1,2,0:T(8,128)} %fusion.142, f32[2,1024,1024]{1,2,0:T(8,128)} %get-tuple-element.366, f32[2,1024]{1,0:T(2,128)S(1)} %get-tuple-element.367), kind=kOutput, calls=%fused_computation.36.clone.1 | convolution fusion | flops 81792000 | bytes 16916480 | tf_op jit(solution)/shard_map/while/body/eval_jaxpr/hqk,khd->qhd/dot_general | solution.py:89
  604.2 12.1 %fusion.145 = bf16[2,16,1024]{2,1,0:T(8,128)(2,1)S(1)} fusion(bf16[1024,2,16]{0,2,1:T(8,128)(2,1)S(1)} %bitcast.217, f32[2,1024,1024]{1,2,0:T(8,128)} %fusion.142, f32[2,1024,1024]{1,2,0:T(8,128)} %get-tuple-element.366, f32[2,1024]{1,0:T(2,128)S(1)} %get-tuple-element.367), kind=kOutput, calls=%fused_computation.35.clone.1 | convolution fusion | flops 81792000 | bytes 16916480 | tf_op jit(solution)/shard_map/while/body/eval_jaxpr/hqk,qhd->khd/dot_general | solution.py:92
  616.3 13.3 %fusion.144 = bf16[2,16,1024]{2,1,0:T(8,128)(2,1)S(1)} fusion(bf16[1024,2,16]{0,2,1:T(8,128)(2,1)S(1)} %bitcast.215, f32[2,1024,1024]{1,2,0:T(8,128)} %fusion.142, f32[2,1024,1024]{1,2,0:T(8,128)} %get-tuple-element.366, f32[2,1024]{1,0:T(2,128)S(1)} %get-tuple-element.367), kind=kOutput, calls=%fused_computation.36.clone.1 | convolution fusion | flops 81792000 | bytes 16916480 | tf_op jit(solution)/shard_map/while/body/eval_jaxpr/hqk,khd->qhd/dot_general | solution.py:89
  647.7 12.1 %fusion.145 = bf16[2,16,1024]{2,1,0:T(8,128)(2,1)S(1)} fusion(bf16[1024,2,16]{0,2,1:T(8,128)(2,1)S(1)} %bitcast.217, f32[2,1024,1024]{1,2,0:T(8,128)} %fusion.142, f32[2,1024,1024]{1,2,0:T(8,128)} %get-tuple-element.366, f32[2,1024]{1,0:T(2,128)S(1)} %get-tuple-element.367), kind=kOutput, calls=%fused_computation.35.clone.1 | convolution fusion | flops 81792000 | bytes 16916480 | tf_op jit(solution)/shard_map/while/body/eval_jaxpr/hqk,qhd->khd/dot_general | solution.py:92
  659.8 13.3 %fusion.144 = bf16[2,16,1024]{2,1,0:T(8,128)(2,1)S(1)} fusion(bf16[1024,2,16]{0,2,1:T(8,128)(2,1)S(1)} %bitcast.215, f32[2,1024,1024]{1,2,0:T(8,128)} %fusion.142, f32[2,1024,1024]{1,2,0:T(8,128)} %get-tuple-element.366, f32[2,1024]{1,0:T(2,128)S(1)} %get-tuple-element.367), kind=kOutput, calls=%fused_computation.36.clone.1 | convolution fusion | flops 81792000 | bytes 16916480 | tf_op jit(solution)/shard_map/while/body/eval_jaxpr/hqk,khd->qhd/dot_general | solution.py:89
  680.5 6.2 fusion.143
  691.2 12.1 %fusion.145 = bf16[2,16,1024]{2,1,0:T(8,128)(2,1)S(1)} fusion(bf16[1024,2,16]{0,2,1:T(8,128)(2,1)S(1)} %bitcast.217, f32[2,1024,1024]{1,2,0:T(8,128)} %fusion.142, f32[2,1024,1024]{1,2,0:T(8,128)} %get-tuple-element.366, f32[2,1024]{1,0:T(2,128)S(1)} %get-tuple-element.367), kind=kOutput, calls=%fused_computation.35.clone.1 | convolution fusion | flops 81792000 | bytes 16916480 | tf_op jit(solution)/shard_map/while/body/eval_jaxpr/hqk,qhd->khd/dot_general | solution.py:92
  703.3 13.3 %fusion.144 = bf16[2,16,1024]{2,1,0:T(8,128)(2,1)S(1)} fusion(bf16[1024,2,16]{0,2,1:T(8,128)(2,1)S(1)} %bitcast.215, f32[2,1024,1024]{1,2,0:T(8,128)} %fusion.142, f32[2,1024,1024]{1,2,0:T(8,128)} %get-tuple-element.366, f32[2,1024]{1,0:T(2,128)S(1)} %get-tuple-element.367), kind=kOutput, calls=%fused_computation.36.clone.1 | convolution fusion | flops 81792000 | bytes 16916480 | tf_op jit(solution)/shard_map/while/body/eval_jaxpr/hqk,khd->qhd/dot_general | solution.py:89
  724.0 6.2 fusion.143
  734.6 12.1 %fusion.145 = bf16[2,16,1024]{2,1,0:T(8,128)(2,1)S(1)} fusion(bf16[1024,2,16]{0,2,1:T(8,128)(2,1)S(1)} %bitcast.217, f32[2,1024,1024]{1,2,0:T(8,128)} %fusion.142, f32[2,1024,1024]{1,2,0:T(8,128)} %get-tuple-element.366, f32[2,1024]{1,0:T(2,128)S(1)} %get-tuple-element.367), kind=kOutput, calls=%fused_computation.35.clone.1 | convolution fusion | flops 81792000 | bytes 16916480 | tf_op jit(solution)/shard_map/while/body/eval_jaxpr/hqk,qhd->khd/dot_general | solution.py:92
  746.7 13.3 %fusion.144 = bf16[2,16,1024]{2,1,0:T(8,128)(2,1)S(1)} fusion(bf16[1024,2,16]{0,2,1:T(8,128)(2,1)S(1)} %bitcast.215, f32[2,1024,1024]{1,2,0:T(8,128)} %fusion.142, f32[2,1024,1024]{1,2,0:T(8,128)} %get-tuple-element.366, f32[2,1024]{1,0:T(2,128)S(1)} %get-tuple-element.367), kind=kOutput, calls=%fused_computation.36.clone.1 | convolution fusion | flops 81792000 | bytes 16916480 | tf_op jit(solution)/shard_map/while/body/eval_jaxpr/hqk,khd->qhd/dot_general | solution.py:89
  778.1 12.1 %fusion.145 = bf16[2,16,1024]{2,1,0:T(8,128)(2,1)S(1)} fusion(bf16[1024,2,16]{0,2,1:T(8,128)(2,1)S(1)} %bitcast.217, f32[2,1024,1024]{1,2,0:T(8,128)} %fusion.142, f32[2,1024,1024]{1,2,0:T(8,128)} %get-tuple-element.366, f32[2,1024]{1,0:T(2,128)S(1)} %get-tuple-element.367), kind=kOutput, calls=%fused_computation.35.clone.1 | convolution fusion | flops 81792000 | bytes 16916480 | tf_op jit(solution)/shard_map/while/body/eval_jaxpr/hqk,qhd->khd/dot_general | solution.py:92
  790.2 13.3 %fusion.144 = bf16[2,16,1024]{2,1,0:T(8,128)(2,1)S(1)} fusion(bf16[1024,2,16]{0,2,1:T(8,128)(2,1)S(1)} %bitcast.215, f32[2,1024,1024]{1,2,0:T(8,128)} %fusion.142, f32[2,1024,1024]{1,2,0:T(8,128)} %get-tuple-element.366, f32[2,1024]{1,0:T(2,128)S(1)} %get-tuple-element.367), kind=kOutput, calls=%fused_computation.36.clone.1 | convolution fusion | flops 81792000 | bytes 16916480 | tf_op jit(solution)/shard_map/while/body/eval_jaxpr/hqk,khd->qhd/dot_general | solution.py:89
  821.6 12.1 %fusion.145 = bf16[2,16,1024]{2,1,0:T(8,128)(2,1)S(1)} fusion(bf16[1024,2,16]{0,2,1:T(8,128)(2,1)S(1)} %bitcast.217, f32[2,1024,1024]{1,2,0:T(8,128)} %fusion.142, f32[2,1024,1024]{1,2,0:T(8,128)} %get-tuple-element.366, f32[2,1024]{1,0:T(2,128)S(1)} %get-tuple-element.367), kind=kOutput, calls=%fused_computation.35.clone.1 | convolution fusion | flops 81792000 | bytes 16916480 | tf_op jit(solution)/shard_map/while/body/eval_jaxpr/hqk,qhd->khd/dot_general | solution.py:92
  833.7 13.3 %fusion.144 = bf16[2,16,1024]{2,1,0:T(8,128)(2,1)S(1)} fusion(bf16[1024,2,16]{0,2,1:T(8,128)(2,1)S(1)} %bitcast.215, f32[2,1024,1024]{1,2,0:T(8,128)} %fusion.142, f32[2,1024,1024]{1,2,0:T(8,128)} %get-tuple-element.366, f32[2,1024]{1,0:T(2,128)S(1)} %get-tuple-element.367), kind=kOutput, calls=%fused_computation.36.clone.1 | convolution fusion | flops 81792000 | bytes 16916480 | tf_op jit(solution)/shard_map/while/body/eval_jaxpr/hqk,khd->qhd/dot_general | solution.py:89
  865.0 12.1 %fusion.145 = bf16[2,16,1024]{2,1,0:T(8,128)(2,1)S(1)} fusion(bf16[1024,2,16]{0,2,1:T(8,128)(2,1)S(1)} %bitcast.217, f32[2,1024,1024]{1,2,0:T(8,128)} %fusion.142, f32[2,1024,1024]{1,2,0:T(8,128)} %get-tuple-element.366, f32[2,1024]{1,0:T(2,128)S(1)} %get-tuple-element.367), kind=kOutput, calls=%fused_computation.35.clone.1 | convolution fusion | flops 81792000 | bytes 16916480 | tf_op jit(solution)/shard_map/while/body/eval_jaxpr/hqk,qhd->khd/dot_general | solution.py:92
  877.1 13.3 %fusion.144 = bf16[2,16,1024]{2,1,0:T(8,128)(2,1)S(1)} fusion(bf16[1024,2,16]{0,2,1:T(8,128)(2,1)S(1)} %bitcast.215, f32[2,1024,1024]{1,2,0:T(8,128)} %fusion.142, f32[2,1024,1024]{1,2,0:T(8,128)} %get-tuple-element.366, f32[2,1024]{1,0:T(2,128)S(1)} %get-tuple-element.367), kind=kOutput, calls=%fused_computation.36.clone.1 | convolution fusion | flops 81792000 | bytes 16916480 | tf_op jit(solution)/shard_map/while/body/eval_jaxpr/hqk,khd->qhd/dot_general | solution.py:89
  908.5 12.1 %fusion.145 = bf16[2,16,1024]{2,1,0:T(8,128)(2,1)S(1)} fusion(bf16[1024,2,16]{0,2,1:T(8,128)(2,1)S(1)} %bitcast.217, f32[2,1024,1024]{1,2,0:T(8,128)} %fusion.142, f32[2,1024,1024]{1,2,0:T(8,128)} %get-tuple-element.366, f32[2,1024]{1,0:T(2,128)S(1)} %get-tuple-element.367), kind=kOutput, calls=%fused_computation.35.clone.1 | convolution fusion | flops 81792000 | bytes 16916480 | tf_op jit(solution)/shard_map/while/body/eval_jaxpr/hqk,qhd->khd/dot_general | solution.py:92
  920.6 13.3 %fusion.144 = bf16[2,16,1024]{2,1,0:T(8,128)(2,1)S(1)} fusion(bf16[1024,2,16]{0,2,1:T(8,128)(2,1)S(1)} %bitcast.215, f32[2,1024,1024]{1,2,0:T(8,128)} %fusion.142, f32[2,1024,1024]{1,2,0:T(8,128)} %get-tuple-element.366, f32[2,1024]{1,0:T(2,128)S(1)} %get-tuple-element.367), kind=kOutput, calls=%fused_computation.36.clone.1 | convolution fusion | flops 81792000 | bytes 16916480 | tf_op jit(solution)/shard_map/while/body/eval_jaxpr/hqk,khd->qhd/dot_general | solution.py:89
  952.0 12.1 %fusion.145 = bf16[2,16,1024]{2,1,0:T(8,128)(2,1)S(1)} fusion(bf16[1024,2,16]{0,2,1:T(8,128)(2,1)S(1)} %bitcast.217, f32[2,1024,1024]{1,2,0:T(8,128)} %fusion.142, f32[2,1024,1024]{1,2,0:T(8,128)} %get-tuple-element.366, f32[2,1024]{1,0:T(2,128)S(1)} %get-tuple-element.367), kind=kOutput, calls=%fused_computation.35.clone.1 | convolution fusion | flops 81792000 | bytes 16916480 | tf_op jit(solution)/shard_map/while/body/eval_jaxpr/hqk,qhd->khd/dot_general | solution.py:92
  964.1 13.3 %fusion.144 = bf16[2,16,1024]{2,1,0:T(8,128)(2,1)S(1)} fusion(bf16[1024,2,16]{0,2,1:T(8,128)(2,1)S(1)} %bitcast.215, f32[2,1024,1024]{1,2,0:T(8,128)} %fusion.142, f32[2,1024,1024]{1,2,0:T(8,128)} %get-tuple-element.366, f32[2,1024]{1,0:T(2,128)S(1)} %get-tuple-element.367), kind=kOutput, calls=%fused_computation.36.clone.1 | convolution fusion | flops 81792000 | bytes 16916480 | tf_op jit(solution)/shard_map/while/body/eval_jaxpr/hqk,khd->qhd/dot_general | solution.py:89
  995.4 12.1 %fusion.145 = bf16[2,16,1024]{2,1,0:T(8,128)(2,1)S(1)} fusion(bf16[1024,2,16]{0,2,1:T(8,128)(2,1)S(1)} %bitcast.217, f32[2,1024,1024]{1,2,0:T(8,128)} %fusion.142, f32[2,1024,1024]{1,2,0:T(8,128)} %get-tuple-element.366, f32[2,1024]{1,0:T(2,128)S(1)} %get-tuple-element.367), kind=kOutput, calls=%fused_computation.35.clone.1 | convolution fusion | flops 81792000 | bytes 16916480 | tf_op jit(solution)/shard_map/while/body/eval_jaxpr/hqk,qhd->khd/dot_general | solution.py:92
  1007.5 13.3 %fusion.144 = bf16[2,16,1024]{2,1,0:T(8,128)(2,1)S(1)} fusion(bf16[1024,2,16]{0,2,1:T(8,128)(2,1)S(1)} %bitcast.215, f32[2,1024,1024]{1,2,0:T(8,128)} %fusion.142, f32[2,1024,1024]{1,2,0:T(8,128)} %get-tuple-element.366, f32[2,1024]{1,0:T(2,128)S(1)} %get-tuple-element.367), kind=kOutput, calls=%fused_computation.36.clone.1 | convolution fusion | flops 81792000 | bytes 16916480 | tf_op jit(solution)/shard_map/while/body/eval_jaxpr/hqk,khd->qhd/dot_general | solution.py:89
  1046.4 26.9 %all-to-all-done.6 = bf16[8,128,1536]{2,1,0:T(8,128)(2,1)} async-done(((bf16[8,128,1536]{2,1,0:T(8,128)(2,1)}), bf16[8,128,1536]{2,1,0:T(8,128)(2,1)}, u32[]{:S(2)}, u32[]{:S(2)}) %all-to-all-start.6) | async-done | bytes 3145760 | tf_op jit(solution)/shard_map/all_to_all | solution.py:174
  1084.9 13.4 %collective-permute-done.1 = bf16[1,512,512]{1,2,0:T(8,128)(2,1)S(1)} collective-permute-done((bf16[1,512,512]{1,2,0:T(8,128)(2,1)S(1)}, bf16[1,512,512]{1,2,0:T(8,128)(2,1)S(1)}, u32[]{:S(2)}, u32[]{:S(2)}) %collective-permute-start.1) | collective-permute-done | bytes 524320 | tf_op jit(solution)/shard_map/ppermute | solution.py:19
  (299 shorter events, 531.2 us)
Async XLA Ops:
  0.6 7.7 copy-start
  0.6 8.3 copy-start.12
  0.7 8.8 copy-start.24
  2.2 0.6 copy-start.14
  3.6 24.5 %all-to-all-start.4 = ((bf16[8,1,128]{2,1,0:T(2,128)(2,1)}), bf16[8,1,128]{2,1,0:T(2,128)(2,1)S(1)}, u32[]{:S(2)}, u32[]{:S(2)}) async-start(bf16[8,1,128]{2,1,0:T(2,128)(2,1)} %compare_convert_fusion), calls=%async_computation.4 | async-start | bytes 8192 | tf_op jit(solution)/shard_map/all_to_all | solution.py:161
  8.0 0.9 copy-start.20
  8.6 3.4 copy-start.2
  8.7 0.8 copy-start.10
  8.9 0.6 copy-start.18
  8.9 0.6 copy-start.16
  17.6 4.0 copy-start.4
  17.6 4.0 copy-start.8
  22.1 10.1 copy-start.6
  28.0 7.3 all-to-all-start.1
  35.4 18.8 %all-to-all-start.5 = ((bf16[8,128,512]{2,1,0:T(8,128)(2,1)}), bf16[8,128,512]{2,1,0:T(8,128)(2,1)S(1)}, u32[]{:S(2)}, u32[]{:S(2)}) async-start(bf16[8,128,512]{2,1,0:T(8,128)(2,1)} %select_select_fusion), calls=%async_computation.5 | async-start | bytes 2097152 | tf_op jit(solution)/shard_map/all_to_all | solution.py:163
  54.2 42.3 %all-to-all-start.3 = ((bf16[8,128,1536]{2,1,0:T(8,128)(2,1)}), bf16[8,128,1536]{2,1,0:T(8,128)(2,1)}, u32[]{:S(2)}, u32[]{:S(2)}) async-start(bf16[8,128,1536]{2,1,0:T(8,128)(2,1)} %broadcast_select_fusion.2), calls=%async_computation.3 | async-start | bytes 6291456 | tf_op jit(solution)/shard_map/all_to_all | solution.py:160
  60.1 8.3 copy-start.22
  96.5 42.3 %all-to-all-start = ((bf16[8,128,1536]{2,1,0:T(8,128)(2,1)}), bf16[8,128,1536]{2,1,0:T(8,128)(2,1)}, u32[]{:S(2)}, u32[]{:S(2)}) async-start(bf16[8,128,1536]{2,1,0:T(8,128)(2,1)} %broadcast_select_fusion.3), calls=%async_computation | async-start | bytes 6291456 | tf_op jit(solution)/shard_map/all_to_all | solution.py:156
  324.1 707.9 %all-to-all-start.2 = ((bf16[8,128,512]{2,1,0:T(8,128)(2,1)}), bf16[8,128,512]{2,1,0:T(8,128)(2,1)}, u32[]{:S(2)}, u32[]{:S(2)}) async-start(bf16[8,128,512]{2,1,0:T(8,128)(2,1)} %bitcast.26), calls=%async_computation.2 | async-start | bytes 2097152 | tf_op jit(solution)/shard_map/all_to_all | solution.py:173
  1032.0 4.8 copy-start.5
  1032.0 5.0 copy-start.15
  1032.0 5.1 copy-start.21
  1032.0 5.9 copy-start.13
  1032.0 5.9 copy-start.23
  1032.0 41.3 %all-to-all-start.6 = ((bf16[8,128,1536]{2,1,0:T(8,128)(2,1)}), bf16[8,128,1536]{2,1,0:T(8,128)(2,1)}, u32[]{:S(2)}, u32[]{:S(2)}) async-start(bf16[8,128,1536]{2,1,0:T(8,128)(2,1)} %bitcast.199), calls=%async_computation.6 | async-start | bytes 6291456 | tf_op jit(solution)/shard_map/all_to_all | solution.py:174
  1036.8 4.6 copy-start.7
  1036.8 4.6 copy-start.9
  1042.7 42.2 %collective-permute-start = (bf16[1,512,512]{2,1,0:T(8,128)(2,1)}, bf16[1,512,512]{2,1,0:T(8,128)(2,1)}, u32[]{:S(2)}, u32[]{:S(2)}) collective-permute-start(bf16[1,512,512]{2,1,0:T(8,128)(2,1)} %fusion.48), channel_id=1, source_target_pairs={{0,8},{8,16},{16,24},{1,9},{9,17},{17,25},{2,10},{10,18},{18,26},{... | collective-permute-start | bytes 1572872 | tf_op jit(solution)/shard_map/ppermute | solution.py:19
  1073.3 6.0 copy-start.3
  1073.3 6.0 copy-start.11
  1073.3 6.0 copy-start.25
  1079.3 2.5 copy-start.19
  1079.3 2.6 copy-start.17
  1081.8 19.3 %copy-start.1 = (bf16[1,4,512,512]{3,2,1,0:T(8,128)(2,1)S(1)}, bf16[1,4,512,512]{3,2,1,0:T(8,128)(2,1)}, u32[]{:S(2)}) copy-start(bf16[1,4,512,512]{3,2,1,0:T(8,128)(2,1)} %param.16) | copy-start | bytes 6291460
  1082.5 15.8 %collective-permute-start.1 = (bf16[1,512,512]{1,2,0:T(8,128)(2,1)S(1)}, bf16[1,512,512]{1,2,0:T(8,128)(2,1)S(1)}, u32[]{:S(2)}, u32[]{:S(2)}) collective-permute-start(bf16[1,512,512]{1,2,0:T(8,128)(2,1)S(1)} %fusion.64), channel_id=1, source_target_pairs={{8,0},{16,8},{24,16},{9,1},{17,9},{25,17},{10,2},{18,10},{26,18},{... | collective-permute-start | bytes 1572872 | tf_op jit(solution)/shard_map/ppermute | solution.py:19
where the time goes:
time: 1110 us; the launch traced here: 1100 us
  matrix products  823 us (74%)
  local copies, waits for them, and re-layouts  108 us (10%)
  waiting for transfers between devices  108 us (10%)
  starting transfers between devices  41.5 us (4%)
  other arithmetic  18.2 us (2%)
    dot_general x16, matrix products, one_block(): jnp.einsum('hqk,khd->qhd', score_grad, key_rows, preferred_element_type=j...  213 us
    sub x32, matrix products, block_probs(): expd = jnp.exp(score - top)  197 us
    dot_general x16, matrix products, one_block(): jnp.einsum('hqk,qhd->khd', score_grad, query, preferred_element_type=jnp....  194 us
    dot_general x16, matrix products, one_block(): jnp.einsum('hqk,qhd->khd', rounded, out_grad, preferred_element_type=jnp....  73.1 us
    dot_general x16, matrix products, one_block(): jnp.einsum('qhd,khd->hqk', out_grad, value_rows, preferred_element_type=j...  72 us
    dot_general x16, matrix products, one_block(): jnp.einsum('hqk,khd->qhd', probs, value_rows, preferred_element_type=jnp....  64.8 us
    all_to_all x1, waiting for transfers between devices, on_device(): lax.all_to_all(send_rows, 'space', split_axis=0, concat_axis=0, tiled=True)  31.3 us
    all_to_all x1, waiting for transfers between devices, on_device(): lax.all_to_all(slot_qkv, 'space', split_axis=0, concat_axis=0, tiled=True)  26.9 us
  transfers between devices with their start and end apart: 9, of which 6 were waited for; matrix products, arithmetic and copies ran while one was open for 69% of the time, Pallas kernels for 0%

commit v1 on v0

v1 whole, which is shorter than its diff:
```python
import functools
import math

import jax
import jax.numpy as jnp
from jax import lax
from jax.experimental import pallas as pl
from jax.experimental.pallas import tpu as pltpu
from jax.sharding import PartitionSpec as P

HEADS = 32
EPS = 1e-05
NEG = -1e30
QT = 128
KT = 256
PATCH = 1024
VMEM_LIMIT = 56 * 1024 * 1024
F32 = jnp.float32
BF16 = jnp.bfloat16
NT = (((1,), (1,)), ((), ()))
NN = (((1,), (0,)), ((), ()))


def dot(a, b, dims=NN):
    return lax.dot_general(a, b, dims, preferred_element_type=F32)


def passed_along(value, axis, by):
    size = lax.axis_size(axis)
    pairs = [(i, i + by) for i in range(size) if 0 <= i + by < size]
    return lax.ppermute(value, axis, pairs)


def centered(values):
    center = values - jnp.mean(values, axis=-1, keepdims=True)
    spread = jnp.mean(center * center, axis=-1, keepdims=True)
    return center, lax.rsqrt(spread + EPS)


def project_kernel(groups, hw, rows_ref, gain_ref, wqkv_ref, out_ref, y_ref):
    width = rows_ref.shape[1]
    center, inv = centered(rows_ref[...].astype(F32))
    normed = (center * inv * gain_ref[...]).astype(BF16)
    y_ref[...] = dot(normed, wqkv_ref[...]).astype(BF16)
    for g in range(groups):
        out_ref[g, :, 0:hw] = y_ref[:, width + g * hw:width + (g + 1) * hw]
        out_ref[g, :, hw:2 * hw] = y_ref[:, 2 * width + g * hw:2 * width + (g + 1) * hw]
        out_ref[g, :, 2 * hw:3 * hw] = y_ref[:, g * hw:(g + 1) * hw]


def project_grad_kernel(
    groups, hw, pick_ref, rows_ref, up_ref, gain_ref, wqkv_ref, wproj_ref, out_ref, y_ref, d_ref
):
    width = up_ref.shape[1]
    center, inv = centered(rows_ref[0].astype(F32))
    normed = (center * inv * gain_ref[...]).astype(BF16)
    y_ref[...] = dot(normed, wqkv_ref[...]).astype(BF16)
    d_ref[...] = dot(up_ref[...], wproj_ref[...], NT).astype(BF16)
    for g in range(groups):
        out_ref[g, :, 0:hw] = y_ref[:, width + g * hw:width + (g + 1) * hw]
        out_ref[g, :, hw:2 * hw] = y_ref[:, 2 * width + g * hw:2 * width + (g + 1) * hw]
        out_ref[g, :, 2 * hw:3 * hw] = y_ref[:, g * hw:(g + 1) * hw]
        out_ref[g, :, 3 * hw:4 * hw] = d_ref[:, g * hw:(g + 1) * hw]


def stacked(tile, head_dim, heads, offset):
    lane = lax.broadcasted_iota(jnp.int32, tile.shape, 1)
    zero = jnp.zeros_like(tile)
    parts = []
    for h in range(heads):
        low = offset + h * head_dim
        parts.append(jnp.where((lane >= low) & (lane < low + head_dim), tile, zero))
    return jnp.concatenate(parts, axis=0)


def own_blocks(wide, head_dim, heads):
    picked = [
        wide[h * head_dim:(h + 1) * head_dim, h * QT:(h + 1) * QT] for h in range(heads)
    ]
    return jnp.concatenate(picked, axis=0).T


def each_block(n_blocks, per_group, blk, body):
    def step(b, carry):
        body(b, b // per_group, pl.multiple_of((b % per_group) * blk, blk))
        return carry

    lax.fori_loop(0, n_blocks, step, 0)


def each_patch(groups, blk, start_ref, body):
    def step(o, carry):
        first = start_ref[o]
        live = (start_ref[o + 1] - first) * blk
        base = pl.multiple_of(first * blk, blk)
        for slots in range(KT, PATCH + 1, KT):
            @pl.when((live > slots - KT) & (live <= slots))
            def _():
                body(slots, base, live)

        return carry

    lax.fori_loop(0, groups, step, 0)


def probs_of(scores, live):
    tiles = list(scores)
    low = (len(tiles) - 1) * KT
    row = lax.broadcasted_iota(jnp.int32, tiles[-1].shape, 0) + low
    tiles[-1] = jnp.where(row < live, tiles[-1], NEG)
    top = functools.reduce(jnp.maximum, [jnp.max(t, axis=0, keepdims=True) for t in tiles])
    expd = [jnp.exp(t - top) for t in tiles]
    total = functools.reduce(jnp.add, [jnp.sum(t, axis=0, keepdims=True) for t in expd])
    inv = 1.0 / total
    return [t * inv for t in expd]


def attend_kernel(
    groups, blk, hw, head_dim, pos_ref, start_ref, x_ref, out_ref, kv, qs, res, kvt, pb
):
    heads = hw // head_dim
    scale = 1.0 / math.sqrt(head_dim)
    rows = x_ref.shape[1]
    per_group = rows // blk
    total = groups * rows

    kv[pl.ds(total, KT), :] = jnp.zeros((KT, 2 * hw), BF16)
    qs[pl.ds(total, KT), :] = jnp.zeros((KT, hw), BF16)

    def place(b, g, r):
        to = pl.multiple_of(pos_ref[b] * blk, blk)
        kv[pl.ds(to, blk), :] = x_ref[g, pl.ds(r, blk), 0:2 * hw]
        qs[pl.ds(to, blk), :] = x_ref[g, pl.ds(r, blk), 2 * hw:3 * hw]

    each_block(groups * per_group, per_group, blk, place)

    def patch(slots, base, live):
        kvt[:, 0:slots] = kv[pl.ds(base, slots), :].T

        def chunk(c, carry):
            at = pl.multiple_of(base + c * QT, blk)
            q = (qs[pl.ds(at, QT), :].astype(F32) * scale).astype(BF16)
            q_st = stacked(q, head_dim, heads, 0)
            if hw < kv.shape[1]:
                q_st = jnp.concatenate([q_st, jnp.zeros_like(q_st)], axis=1)
            scores = [
                dot(kv[pl.ds(pl.multiple_of(base + t, blk), KT), :], q_st, NT)
                for t in range(0, slots, KT)
            ]
            for t, p in enumerate(probs_of(scores, live)):
                pb[t * KT:(t + 1) * KT, :] = p.astype(BF16)
            wide = dot(kvt[hw:2 * hw, 0:slots], pb[0:slots, :])
            res[pl.ds(at, QT), :] = own_blocks(wide, head_dim, heads).astype(BF16)
            return carry

        lax.fori_loop(0, (live + QT - 1) // QT, chunk, 0)

    each_patch(groups, blk, start_ref, patch)

    def back(b, g, r):
        at = pl.multiple_of(pos_ref[b] * blk, blk)
        out_ref[g, pl.ds(r, blk), :] = res[pl.ds(at, blk), :]

    each_block(groups * per_group, per_group, blk, back)


def attend_grad_kernel(
    groups, blk, hw, head_dim, pos_ref, start_ref, x_ref, out_ref, kv, qd, dq, dkv, kvt, both, acc
):
    heads = hw // head_dim
    scale = 1.0 / math.sqrt(head_dim)
    rows = x_ref.shape[1]
    per_group = rows // blk
    total = groups * rows
    span = heads * QT

    kv[pl.ds(total, KT), :] = jnp.zeros((KT, 2 * hw), BF16)
    qd[pl.ds(total, KT), :] = jnp.zeros((KT, 2 * hw), BF16)

    def place(b, g, r):
        to = pl.multiple_of(pos_ref[b] * blk, blk)
        kv[pl.ds(to, blk), :] = x_ref[g, pl.ds(r, blk), 0:2 * hw]
        qd[pl.ds(to, blk), :] = x_ref[g, pl.ds(r, blk), 2 * hw:4 * hw]

    each_block(groups * per_group, per_group, blk, place)

    def patch(slots, base, live):
        kvt[:, 0:slots] = kv[pl.ds(base, slots), :].T
        acc[0:slots, :] = jnp.zeros((slots, 2 * hw), F32)

        def chunk(c, carry):
            at = pl.multiple_of(base + c * QT, blk)
            tile = qd[pl.ds(at, QT), :]
            q_st = stacked((tile.astype(F32) * scale).astype(BF16), head_dim, heads, 0)
            row = lax.broadcasted_iota(jnp.int32, tile.shape, 0) + c * QT
            d_st = stacked(jnp.where(row < live, tile, jnp.zeros_like(tile)), head_dim, heads, hw)
            keys = [
                kv[pl.ds(pl.multiple_of(base + t, blk), KT), :] for t in range(0, slots, KT)
            ]
            probs = probs_of([dot(k, q_st, NT) for k in keys], live)
            grads = [dot(k, d_st, NT) for k in keys]
            delta = functools.reduce(
                jnp.add, [jnp.sum(p * g, axis=0, keepdims=True) for p, g in zip(probs, grads)]
            )
            for t, (p, g) in enumerate(zip(probs, grads)):
                both[t * KT:(t + 1) * KT, 0:span] = (p * (g - delta)).astype(BF16)
                both[t * KT:(t + 1) * KT, span:2 * span] = p.astype(BF16)
            right = jnp.concatenate([q_st, d_st], axis=0)
            acc[0:slots, :] += dot(both[0:slots, :], right)
            wide = dot(kvt[0:hw, 0:slots], both[0:slots, 0:span]) * scale
            dq[pl.ds(at, QT), :] = own_blocks(wide, head_dim, heads).astype(BF16)
            return carry

        lax.fori_loop(0, (live + QT - 1) // QT, chunk, 0)
        dkv[pl.ds(base, slots), :] = acc[0:slots, :].astype(BF16)

    each_patch(groups, blk, start_ref, patch)

    def back(b, g, r):
        at = pl.multiple_of(pos_ref[b] * blk, blk)
        out_ref[g, pl.ds(r, blk), 0:2 * hw] = dkv[pl.ds(at, blk), :]
        out_ref[g, pl.ds(r, blk), 2 * hw:3 * hw] = dq[pl.ds(at, blk), :]

    each_block(groups * per_group, per_group, blk, back)


def mix_kernel(groups, hw, att_ref, rows_ref, wproj_ref, out_ref, a_ref):
    for g in range(groups):
        a_ref[:, g * hw:(g + 1) * hw] = att_ref[g]
    mixed = rows_ref[...].astype(F32) + dot(a_ref[...], wproj_ref[...])
    out_ref[...] = mixed.astype(BF16)


def input_grad_kernel(
    groups, hw, pick_ref, dqkv_ref, rows_ref, up_ref, gain_ref, wqkv_ref, out_ref, y_ref
):
    width = up_ref.shape[1]
    for g in range(groups):
        y_ref[:, width + g * hw:width + (g + 1) * hw] = dqkv_ref[g, :, 0:hw]
        y_ref[:, 2 * width + g * hw:2 * width + (g + 1) * hw] = dqkv_ref[g, :, hw:2 * hw]
        y_ref[:, g * hw:(g + 1) * hw] = dqkv_ref[g, :, 2 * hw:3 * hw]
    grad = dot(y_ref[...], wqkv_ref[...], NT) * gain_ref[...]
    center, inv = centered(rows_ref[0].astype(F32))
    unit = center * inv
    mean = jnp.mean(grad, axis=-1, keepdims=True)
    along = jnp.mean(grad * unit, axis=-1, keepdims=True)
    pulled = inv * (grad - mean - unit * along)
    out_ref[...] = (up_ref[...].astype(F32) + pulled).astype(BF16)


def call(kernel, out_shape, operands, scratch=(), smem=0, cost=None, name=None, picked=None):
    specs = [pl.BlockSpec(memory_space=pltpu.SMEM)] * smem
    specs += [pl.BlockSpec(memory_space=pltpu.VMEM)] * (len(operands) - smem)
    kwargs = dict(
        out_shape=jax.ShapeDtypeStruct(out_shape, BF16),
        cost_estimate=pl.CostEstimate(flops=cost[0], bytes_accessed=cost[1], transcendentals=0),
        compiler_params=pltpu.CompilerParams(vmem_limit_bytes=VMEM_LIMIT),
        name=name,
    )
    if picked is None:
        return pl.pallas_call(
            kernel,
            in_specs=specs,
            out_specs=pl.BlockSpec(memory_space=pltpu.VMEM),
            scratch_shapes=list(scratch),
            **kwargs,
        )(*operands)

    def whole(shape):
        return pl.BlockSpec(shape, lambda i, pick: (0,) * len(shape))

    specs = [whole(o.shape) for o in operands[1:]]
    stash = operands[picked]
    specs[picked - 1] = pl.BlockSpec((1,) + stash.shape[1:], lambda i, pick: (pick[0], 0, 0))
    return pl.pallas_call(
        kernel,
        grid_spec=pltpu.PrefetchScalarGridSpec(
            num_scalar_prefetch=1,
            grid=(1,),
            in_specs=specs,
            out_specs=whole(out_shape),
            scratch_shapes=list(scratch),
        ),
        **kwargs,
    )(*operands)


def places(owners, groups):
    count = owners.shape[0]
    key = owners * count + jnp.arange(count, dtype=jnp.int32)
    pos = jnp.sum((key[None, :] < key[:, None]).astype(jnp.int32), axis=1)
    bounds = jnp.arange(groups + 1, dtype=jnp.int32)
    start = jnp.sum((owners[None, :] < bounds[:, None]).astype(jnp.int32), axis=1)
    return pos, start


def swap(value):
    return lax.all_to_all(value, "space", split_axis=0, concat_axis=0, tiled=True)


def on_device(
    act_in, stash, plan, grad_in, fwd_owner, stash_owner, ln_gain, qkv_weight, proj_weight
):
    groups = lax.axis_size("space")
    rows_in = act_in[0]
    rows, width = rows_in.shape
    head_dim = width // HEADS
    hw = width // groups
    blk = rows // groups
    heads = hw // head_dim
    total = groups * rows
    span = heads * QT
    w_qkv = qkv_weight[0]
    w_proj = proj_weight[0]
    stored = stash[0]
    upstream = grad_in[0]
    stored_owners = lax.dynamic_index_in_dim(stash_owner[0], plan[0], 0, keepdims=False)
    mine = jnp.stack([fwd_owner[0][::blk], stored_owners[::blk]])
    owners = lax.all_gather(mine, "space", axis=0)
    pos, start = places(owners[:, 0].reshape(-1), groups)
    pos_b, start_b = places(owners[:, 1].reshape(-1), groups)

    sent = call(
        functools.partial(project_kernel, groups, hw),
        (groups, rows, 3 * hw),
        (rows_in, ln_gain, w_qkv),
        [pltpu.VMEM((rows, 3 * width), BF16)],
        cost=(6 * rows * width * width, 5 * 1024 * 1024),
        name="project",
    )
    sent_b = call(
        functools.partial(project_grad_kernel, groups, hw),
        (groups, rows, 4 * hw),
        (plan, stored, upstream, ln_gain, w_qkv, w_proj),
        [pltpu.VMEM((rows, 3 * width), BF16), pltpu.VMEM((rows, width), BF16)],
        cost=(8 * rows * width * width, 6 * 1024 * 1024),
        name="project_grad",
        picked=1,
    )
    got = swap(sent)
    got_b = swap(sent_b)
    attended = call(
        functools.partial(attend_kernel, groups, blk, hw, head_dim),
        (groups, rows, hw),
        (pos, start, got),
        [
            pltpu.VMEM((total + KT, 2 * hw), BF16),
            pltpu.VMEM((total + KT, hw), BF16),
            pltpu.VMEM((total + KT, hw), BF16),
            pltpu.VMEM((2 * hw, PATCH), BF16),
            pltpu.VMEM((PATCH, span), BF16),
        ],
        smem=2,
        cost=(10_000_000_000, 3 * 1024 * 1024),
        name="attend",
    )
    ret = swap(attended)
    grads = call(
        functools.partial(attend_grad_kernel, groups, blk, hw, head_dim),
        (groups, rows, 3 * hw),
        (pos_b, start_b, got_b),
        [
            pltpu.VMEM((total + KT, 2 * hw), BF16),
            pltpu.VMEM((total + KT, 2 * hw), BF16),
            pltpu.VMEM((total + KT, hw), BF16),
            pltpu.VMEM((total + KT, 2 * hw), BF16),
            pltpu.VMEM((2 * hw, PATCH), BF16),
            pltpu.VMEM((PATCH, 2 * span), BF16),
            pltpu.VMEM((PATCH, 2 * hw), F32),
        ],
        smem=2,
        cost=(30_000_000_000, 4 * 1024 * 1024),
        name="attend_grad",
    )
    ret_grads = swap(grads)
    mixed = call(
        functools.partial(mix_kernel, groups, hw),
        (rows, width),
        (ret, rows_in, w_proj),
        [pltpu.VMEM((rows, width), BF16)],
        cost=(2 * rows * width * width, 2 * 1024 * 1024),
        name="mix",
    )
    act_out = passed_along(mixed[None], "section", 1)
    input_grad = call(
        functools.partial(input_grad_kernel, groups, hw),
        (rows, width),
        (plan, ret_grads, stored, upstream, ln_gain, w_qkv),
        [pltpu.VMEM((rows, 3 * width), BF16)],
        cost=(6 * rows * width * width, 5 * 1024 * 1024),
        name="input_grad",
        picked=2,
    )
    grad_out = passed_along(input_grad[None], "section", -1)
    return (act_out, grad_out)


def solution(mesh):
    in_specs = (
        P("section", "space", None),
        P("section", None, "space", None),
        P("section"),
        P("section", "space", None),
        P("section", "space"),
        P("section", None, "space"),
        P("section", None),
        P("section", None, None),
        P("section", None, None),
    )
    out_specs = (P("section", "space", None), P("section", "space", None))
    return jax.shard_map(
        on_device, mesh=mesh, in_specs=in_specs, out_specs=out_specs, check_vma=False
    )
```

time: 1110 us -> 220 us (0.20)
  matrix products: 823 us -> 0 us
  Pallas kernels: 0 us -> 128 us
  local copies, waits for them, and re-layouts: 108 us -> 18.9 us
  waiting for transfers between devices: 108 us -> 27.5 us
  blocking collectives: 0 us -> 19.8 us
  starting transfers between devices: 41.5 us -> 23.4 us
  other arithmetic: 18.2 us -> 2.7 us
    dot_general x85 -> x0, matrix products: 626 us -> none  [the longest x16 213 us: one_block(): jnp.einsum('hqk,khd->qhd', score_grad, key_rows, preferred_element_type=j...]
    sub x32 -> x0, matrix products: 197 us -> none  [block_probs(): expd = jnp.exp(score - top)]
    pallas_call x0 -> x6, Pallas kernels: none -> 128 us  [the longest x4 118 us: call(): pl.pallas_call(kernel, in_specs=specs, out_specs=pl.BlockSpec(memory_spac...]
    all_to_all x7 -> x4, waiting for transfers between devices: 94.6 us -> 13.4 us  [swap(): lax.all_to_all(value, 'space', split_axis=0, concat_axis=0, tiled=True)]
    dynamic_update_slice x64 -> x0, local copies, waits for them, and re-layouts: 30.4 us -> none  [the longest x16 10.3 us: one_block(): lax.dynamic_update_slice_in_dim(totals, value_grad, 2 * width + start, 1)]
    dynamic_slice x34 -> x1, local copies, waits for them, and re-layouts: 30.3 us -> 0.01 us  [on_device(): lax.dynamic_index_in_dim(stash_owner[0], plan[0], 0, keepdims=False)]
    gather x5 -> x0, local copies, waits for them, and re-layouts: 24.6 us -> none  [the longest x3 15.3 us: pack_rows(): jnp.take(source, index.reshape(-1), axis=0)]
    all_gather x0 -> x1, blocking collectives: none -> 19.8 us  [on_device(): owners = lax.all_gather(mine, 'space', axis=0)]
  transfers between devices with their start and end apart: 9 -> 6, of which waited for: 6 -> 2; matrix products, arithmetic and copies ran while one was open for 69% -> 7% of each run, Pallas kernels for 0% -> 56%
where the time goes in v1:
time: 220 us; the launch traced here: 222 us
  Pallas kernels  128 us (58%)
  waiting for transfers between devices  27.5 us (12%)
  starting transfers between devices  23.4 us (11%)
  blocking collectives  19.8 us (9%)
  local copies, waits for them, and re-layouts  18.9 us (9%)
  other arithmetic  2.7 us (1%)
    pallas_call x4, Pallas kernels, call(): pl.pallas_call(kernel, in_specs=specs, out_specs=pl.BlockSpec(memory_spac...  118 us
    all_gather x1, blocking collectives, on_device(): owners = lax.all_gather(mine, 'space', axis=0)  19.8 us
    all_to_all x4, starting transfers between devices, swap(): lax.all_to_all(value, 'space', split_axis=0, concat_axis=0, tiled=True)  19.6 us
    ppermute x2, waiting for transfers between devices, passed_along(): return lax.ppermute(value, axis, pairs)  14.1 us
    all_to_all x4, waiting for transfers between devices, swap(): lax.all_to_all(value, 'space', split_axis=0, concat_axis=0, tiled=True)  13.4 us
    pallas_call x2, Pallas kernels, call(): pl.pallas_call(kernel, grid_spec=pltpu.PrefetchScalarGridSpec(num_scalar_...  10.1 us
    pallas_call x3, local copies, waits for them, and re-layouts, call(): pl.pallas_call(kernel, in_specs=specs, out_specs=pl.BlockSpec(memory_spac...  10.1 us
    all_to_all x3, local copies, waits for them, and re-layouts, swap(): lax.all_to_all(value, 'space', split_axis=0, concat_axis=0, tiled=True)  6.15 us
  transfers between devices with their start and end apart: 6, of which 2 were waited for; matrix products, arithmetic and copies ran while one was open for 7% of the time, Pallas kernels for 56%

profile of v1, /device:TPU:10, one launch (start us, length us, event | category | flops | bytes accessed | tf_op | source)
XLA Modules:
  0.0 221.9 jit_solution(11614087019646431253)
XLA Ops:
  0.6 0.0 copy-start
  0.6 4.6 %project.1 = bf16[8,512,192]{2,1,0:T(8,128)(2,1)} custom-call(bf16[512,512]{1,0:T(8,128)(2,1)} %bitcast.26, f32[1,512]{1,0:T(1,128)} %gain_ref.5, bf16[512,1536]{1,0:T(8,128)(2,1)} %bitcast.17), custom_call_target="tpu_custom_call" | custom-call | flops 805306368 | bytes 5242880 | tf_op jit(solution)/shard_map/project/pallas_call | solution.py:261
  5.3 3.9 %copy.17 = bf16[8,512,192]{1,2,0:T(8,128)(2,1)} copy(bf16[8,512,192]{2,1,0:T(8,128)(2,1)} %project.1) | data formatting | bytes 3145728 | tf_op jit(solution)/shard_map/project/pallas_call | solution.py:261
  9.1 4.3 %all-to-all-start = ((bf16[8,512,192]{1,2,0:T(8,128)(2,1)}), bf16[8,512,192]{1,2,0:T(8,128)(2,1)S(1)}, u32[]{:S(2)}, u32[]{:S(2)}) async-start(bf16[8,512,192]{1,2,0:T(8,128)(2,1)} %copy.17), calls=%async_computation | async-start | bytes 3145728 | tf_op jit(solution)/shard_map/all_to_all | solution.py:298
  14.1 0.0 copy-done
  14.1 0.1 slice.13
  14.2 0.8 slice.12
  15.0 19.8 %all-gather.1 = s32[8,2,8]{2,1,0:T(2,128)S(1)} all-gather(s32[1,2,8]{2,1,0:T(2,128)S(1)} %add_bitcast_fusion), channel_id=2, replica_groups=mesh['section'=4,'space'=8] {'space'}, dimensions={0}, use_global_device_ids=true | all-gather | bytes 576 | tf_op jit(solution)/shard_map/all_gather | solution.py:319
  34.8 0.1 reshape_squeeze.7
  34.9 0.1 reshape_squeeze.6
  35.0 5.1 %project_grad.1 = bf16[8,512,256]{2,1,0:T(8,128)(2,1)} custom-call(s32[1]{0:T(128)} %copy.25.pick_ref, bf16[4,512,512]{2,1,0:T(8,128)(2,1)} %bitcast.20, bf16[512,512]{1,0:T(8,128)(2,1)} %bitcast.24, f32[1,512]{1,0:T(1,128)} %gain_ref.5, bf16[512,1536]{1,0:T(8,128)(2,1)} %bitcast.18, bf16[512,512]{1,0:T(8,128)(2,1)} %bitcast.22), custom_call_target="tpu_custom_call" | custom-call | flops 1073741824 | bytes 6291456 | tf_op jit(solution)/shard_map/project_grad/pallas_call | solution.py:275
  40.1 0.0 all-to-all-done
  40.1 6.9 %all-to-all-start.2 = ((bf16[8,512,256]{2,1,0:T(8,128)(2,1)}), bf16[8,512,256]{2,1,0:T(8,128)(2,1)}, u32[]{:S(2)}, u32[]{:S(2)}) async-start(bf16[8,512,256]{2,1,0:T(8,128)(2,1)} %project_grad.1), calls=%async_computation.2 | async-start | bytes 4194304 | tf_op jit(solution)/shard_map/all_to_all | solution.py:298
  47.0 0.7 convert_reduce_fusion.2.start_ref
  47.7 0.6 convert_reduce_fusion.3.start_ref
  48.3 0.7 convert_reduce_fusion.pos_ref
  49.0 0.7 convert_reduce_fusion.1.pos_ref
  49.7 2.4 %copy.18.x_ref = bf16[8,512,192]{2,1,0:T(8,128)(2,1)} copy(bf16[8,512,192]{1,2,0:T(8,128)(2,1)S(1)} %all-to-all-done) | data formatting | bytes 3145728 | tf_op jit(solution)/shard_map/all_to_all | solution.py:298
  52.1 42.5 %attend.1 = bf16[8,512,64]{2,1,0:T(8,128)(2,1)} custom-call(s32[64]{0:T(128)} %convert_reduce_fusion.1.pos_ref, s32[9]{0:T(128)} %convert_reduce_fusion.3.start_ref, bf16[8,512,192]{2,1,0:T(8,128)(2,1)} %copy.18.x_ref), custom_call_target="tpu_custom_call" | custom-call | flops 10000000000 | bytes 3145728 | tf_op jit(solution)/shard_map/attend/pallas_call | solution.py:261
  94.6 2.3 %copy.19 = bf16[8,512,64]{1,2,0:T(8,128)(2,1)} copy(bf16[8,512,64]{2,1,0:T(8,128)(2,1)} %attend.1) | data formatting | bytes 1048576 | tf_op jit(solution)/shard_map/attend/pallas_call | solution.py:261
  96.9 0.0 all-to-all-done.2.x_ref
  96.9 4.2 %all-to-all-start.1 = ((bf16[8,512,64]{1,2,0:T(8,128)(2,1)}), bf16[8,512,64]{1,2,0:T(8,128)(2,1)S(1)}, u32[]{:S(2)}, u32[]{:S(2)}) async-start(bf16[8,512,64]{1,2,0:T(8,128)(2,1)} %copy.19), calls=%async_computation.1 | async-start | bytes 1048576 | tf_op jit(solution)/shard_map/all_to_all | solution.py:298
  101.1 68.2 %attend_grad.1 = bf16[8,512,192]{2,1,0:T(8,128)(2,1)} custom-call(s32[64]{0:T(128)} %convert_reduce_fusion.pos_ref, s32[9]{0:T(128)} %convert_reduce_fusion.2.start_ref, bf16[8,512,256]{2,1,0:T(8,128)(2,1)} %all-to-all-done.2.x_ref), custom_call_target="tpu_custom_call" | custom-call | flops 30000001024 | bytes 4194304 | tf_op jit(solution)/shard_map/attend_grad/pallas_call | solution.py:261
  169.4 3.9 %copy.21 = bf16[8,512,192]{1,2,0:T(8,128)(2,1)} copy(bf16[8,512,192]{2,1,0:T(8,128)(2,1)} %attend_grad.1) | data formatting | bytes 3145728 | tf_op jit(solution)/shard_map/attend_grad/pallas_call | solution.py:261
  173.2 0.0 all-to-all-done.1
  173.2 4.2 %all-to-all-start.3 = ((bf16[8,512,192]{1,2,0:T(8,128)(2,1)}), bf16[8,512,192]{1,2,0:T(8,128)(2,1)S(1)}, u32[]{:S(2)}, u32[]{:S(2)}) async-start(bf16[8,512,192]{1,2,0:T(8,128)(2,1)} %copy.21), calls=%async_computation.3 | async-start | bytes 3145728 | tf_op jit(solution)/shard_map/all_to_all | solution.py:298
  177.4 1.3 copy.20.att_ref
  178.7 2.9 %mix.1 = bf16[512,512]{1,0:T(8,128)(2,1)} custom-call(bf16[8,512,64]{2,1,0:T(8,128)(2,1)} %copy.20.att_ref, bf16[512,512]{1,0:T(8,128)(2,1)} %bitcast.27, bf16[512,512]{1,0:T(8,128)(2,1)} %bitcast.23), custom_call_target="tpu_custom_call" | custom-call | flops 268435456 | bytes 2097152 | tf_op jit(solution)/shard_map/mix/pallas_call | solution.py:261
  181.6 1.9 collective-permute-start
  183.5 13.4 %all-to-all-done.3 = bf16[8,512,192]{1,2,0:T(8,128)(2,1)S(1)} async-done(((bf16[8,512,192]{1,2,0:T(8,128)(2,1)}), bf16[8,512,192]{1,2,0:T(8,128)(2,1)S(1)}, u32[]{:S(2)}, u32[]{:S(2)}) %all-to-all-start.3) | async-done | bytes 1572896 | tf_op jit(solution)/shard_map/all_to_all | solution.py:298
  197.0 2.4 %copy.22.dqkv_ref = bf16[8,512,192]{2,1,0:T(8,128)(2,1)} copy(bf16[8,512,192]{1,2,0:T(8,128)(2,1)S(1)} %all-to-all-done.3) | data formatting | bytes 3145728 | tf_op jit(solution)/shard_map/all_to_all | solution.py:298
  199.4 4.9 %input_grad.1 = bf16[512,512]{1,0:T(8,128)(2,1)} custom-call(s32[1]{0:T(128)} %copy.25.pick_ref, bf16[8,512,192]{2,1,0:T(8,128)(2,1)} %copy.22.dqkv_ref, bf16[4,512,512]{2,1,0:T(8,128)(2,1)} %bitcast.21, bf16[512,512]{1,0:T(8,128)(2,1)} %bitcast.25, f32[1,512]{1,0:T(1,128)} %gain_ref.5, bf16[512,1536]{1,0:T(8,128)(2,1)} %bitcast.19), custom_call_target="tpu_custom_call" | custom-call | flops 805306368 | bytes 5242880 | tf_op jit(solution)/shard_map/input_grad/pallas_call | solution.py:275
  204.3 1.9 collective-permute-start.1
  206.2 0.0 collective-permute-done
  206.2 14.1 %collective-permute-done.1 = bf16[1,512,512]{2,1,0:T(8,128)(2,1)S(1)} collective-permute-done((bf16[1,512,512]{2,1,0:T(8,128)(2,1)}, bf16[1,512,512]{2,1,0:T(8,128)(2,1)S(1)}, u32[]{:S(2)}, u32[]{:S(2)}) %collective-permute-start.1) | collective-permute-done | bytes 524320 | tf_op jit(solution)/shard_map/ppermute | solution.py:31
  220.3 0.8 copy.26
  221.1 0.8 copy.27
  (5 shorter events, 0.1 us)
Async XLA Ops:
  0.6 13.4 %copy-start = (s32[1,4,512]{2,1,0:T(4,128)S(1)}, s32[1,4,512]{2,1,0:T(4,128)}, u32[]{:S(2)}) copy-start(s32[1,4,512]{2,1,0:T(4,128)} %param.14) | copy-start | bytes 24580
  9.1 31.0 %all-to-all-start = ((bf16[8,512,192]{1,2,0:T(8,128)(2,1)}), bf16[8,512,192]{1,2,0:T(8,128)(2,1)S(1)}, u32[]{:S(2)}, u32[]{:S(2)}) async-start(bf16[8,512,192]{1,2,0:T(8,128)(2,1)} %copy.17), calls=%async_computation | async-start | bytes 3145728 | tf_op jit(solution)/shard_map/all_to_all | solution.py:298
  40.1 56.8 %all-to-all-start.2 = ((bf16[8,512,256]{2,1,0:T(8,128)(2,1)}), bf16[8,512,256]{2,1,0:T(8,128)(2,1)}, u32[]{:S(2)}, u32[]{:S(2)}) async-start(bf16[8,512,256]{2,1,0:T(8,128)(2,1)} %project_grad.1), calls=%async_computation.2 | async-start | bytes 4194304 | tf_op jit(solution)/shard_map/all_to_all | solution.py:298
  96.9 76.3 %all-to-all-start.1 = ((bf16[8,512,64]{1,2,0:T(8,128)(2,1)}), bf16[8,512,64]{1,2,0:T(8,128)(2,1)S(1)}, u32[]{:S(2)}, u32[]{:S(2)}) async-start(bf16[8,512,64]{1,2,0:T(8,128)(2,1)} %copy.19), calls=%async_computation.1 | async-start | bytes 1048576 | tf_op jit(solution)/shard_map/all_to_all | solution.py:298
  173.2 23.7 %all-to-all-start.3 = ((bf16[8,512,192]{1,2,0:T(8,128)(2,1)}), bf16[8,512,192]{1,2,0:T(8,128)(2,1)S(1)}, u32[]{:S(2)}, u32[]{:S(2)}) async-start(bf16[8,512,192]{1,2,0:T(8,128)(2,1)} %copy.21), calls=%async_computation.3 | async-start | bytes 3145728 | tf_op jit(solution)/shard_map/all_to_all | solution.py:298
  181.6 24.6 %collective-permute-start = (bf16[1,512,512]{2,1,0:T(8,128)(2,1)}, bf16[1,512,512]{2,1,0:T(8,128)(2,1)S(1)}, u32[]{:S(2)}, u32[]{:S(2)}) collective-permute-start(bf16[1,512,512]{2,1,0:T(8,128)(2,1)} %bitcast.28), channel_id=1, source_target_pairs={{0,8},{8,16},{16,24},{1,9},{9,17},{17,25},{2,10},{10,18},{18,26},{... | collective-permute-start | bytes 1572872 | tf_op jit(solution)/shard_map/ppermute | solution.py:31
  204.3 16.0 %collective-permute-start.1 = (bf16[1,512,512]{2,1,0:T(8,128)(2,1)}, bf16[1,512,512]{2,1,0:T(8,128)(2,1)S(1)}, u32[]{:S(2)}, u32[]{:S(2)}) collective-permute-start(bf16[1,512,512]{2,1,0:T(8,128)(2,1)} %bitcast.29), channel_id=1, source_target_pairs={{8,0},{16,8},{24,16},{9,1},{17,9},{25,17},{10,2},{18,10},{26,18},{... | collective-permute-start | bytes 1572872 | tf_op jit(solution)/shard_map/ppermute | solution.py:31

commit v2 on v1

v2 whole, which is shorter than its diff:
```python
import functools
import math

import jax
import jax.numpy as jnp
from jax import lax
from jax.experimental import pallas as pl
from jax.experimental.pallas import tpu as pltpu
from jax.sharding import PartitionSpec as P

HEADS = 32
EPS = 1e-05
NEG = -1e30
QT = 128
KT = 256
PATCH = 1024
VMEM_LIMIT = 56 * 1024 * 1024
F32 = jnp.float32
BF16 = jnp.bfloat16
NT = (((1,), (1,)), ((), ()))
NN = (((1,), (0,)), ((), ()))


def dot(a, b, dims=NN):
    return lax.dot_general(a, b, dims, preferred_element_type=F32)


def passed_along(value, axis, by):
    size = lax.axis_size(axis)
    pairs = [(i, i + by) for i in range(size) if 0 <= i + by < size]
    return lax.ppermute(value, axis, pairs)


def centered(values):
    center = values - jnp.mean(values, axis=-1, keepdims=True)
    spread = jnp.mean(center * center, axis=-1, keepdims=True)
    return center, lax.rsqrt(spread + EPS)


def spread(groups, hw, y_ref, out_ref):
    rows, width = y_ref.shape[0], y_ref.shape[1] // 3
    for g in range(groups):
        low = g * hw
        out_ref[g, 0:rows, 0:hw] = y_ref[:, width + low:width + low + hw]
        out_ref[g, 0:rows, hw:2 * hw] = y_ref[:, 2 * width + low:2 * width + low + hw]


def project_kernel(groups, hw, rows_ref, gain_ref, wqkv_ref, out_ref, y_ref):
    rows = rows_ref.shape[0]
    half = rows // 2
    center, inv = centered(rows_ref[...].astype(F32))
    normed = (center * inv * gain_ref[...]).astype(BF16)
    y_ref[...] = dot(normed, wqkv_ref[...]).astype(BF16)
    spread(groups, hw, y_ref, out_ref)
    for g in range(groups):
        out_ref[g, rows:rows + half, 0:hw] = y_ref[0:half, g * hw:(g + 1) * hw]
        out_ref[g, rows:rows + half, hw:2 * hw] = y_ref[half:rows, g * hw:(g + 1) * hw]


def project_grad_kernel(
    groups,
    hw,
    pick_ref,
    rows_ref,
    up_ref,
    gain_ref,
    wqkv_ref,
    wproj_ref,
    owners_ref,
    out_ref,
    y_ref,
    d_ref,
):
    rows = up_ref.shape[0]
    center, inv = centered(rows_ref[0].astype(F32))
    normed = (center * inv * gain_ref[...]).astype(BF16)
    y_ref[...] = dot(normed, wqkv_ref[...]).astype(BF16)
    d_ref[...] = dot(up_ref[...], wproj_ref[...], NT).astype(BF16)
    spread(groups, hw, y_ref, out_ref)
    for g in range(groups):
        out_ref[g, rows:2 * rows, 0:hw] = y_ref[:, g * hw:(g + 1) * hw]
        out_ref[g, rows:2 * rows, hw:2 * hw] = d_ref[:, g * hw:(g + 1) * hw]
        out_ref[g, 2 * rows:, :] = owners_ref[...]


def stacked(tile, head_dim, heads, offset):
    lane = lax.broadcasted_iota(jnp.int32, tile.shape, 1)
    zero = jnp.zeros_like(tile)
    parts = []
    for h in range(heads):
        low = offset + h * head_dim
        parts.append(jnp.where((lane >= low) & (lane < low + head_dim), tile, zero))
    return jnp.concatenate(parts, axis=0)


def own_blocks(wide, head_dim, heads):
    picked = [
        wide[h * head_dim:(h + 1) * head_dim, h * QT:(h + 1) * QT] for h in range(heads)
    ]
    return jnp.concatenate(picked, axis=0).T


def each_block(groups, per_group, blk, body, first=0, count=None):
    count = per_group if count is None else count

    def step(b, carry):
        g, j = b // count, first + b % count
        body(g * per_group + j, g, pl.multiple_of(j * blk, blk))
        return carry

    lax.fori_loop(0, groups * count, step, 0)


def each_patch(which, groups, blk, at_ref, small, body):
    n_blocks = at_ref.shape[1] - groups - 1

    def step(o, carry):
        first = at_ref[which, n_blocks + o]
        live = (at_ref[which, n_blocks + o + 1] - first) * blk
        base = pl.multiple_of(first * blk, blk)
        for slots in range(KT, PATCH + 1, KT):
            fits = (live > slots - KT) & (live <= slots)

            @pl.when(fits & small)
            def _():
                body(slots, base, live, False)

            @pl.when(fits & jnp.logical_not(small))
            def _():
                body(slots, base, live, True)

        return carry

    lax.fori_loop(0, groups, step, 0)


def largest_norm(tiles, hw, head_dim):
    lanes = 2 * hw
    col = lax.broadcasted_iota(jnp.int32, (lanes, 128), 0)
    head = lax.broadcasted_iota(jnp.int32, (lanes, 128), 1)
    pick = ((col // head_dim == head) & (col < hw)).astype(BF16)
    best = None
    for tile in tiles:
        values = tile.astype(F32)
        norm = jnp.max(dot((values * values).astype(BF16), pick), axis=0, keepdims=True)
        best = norm if best is None else jnp.maximum(best, norm)
    return jnp.max(best)


def probs_of(scores, live, shifted):
    tiles = list(scores)
    low = (len(tiles) - 1) * KT
    row = lax.broadcasted_iota(jnp.int32, tiles[-1].shape, 0) + low
    tiles[-1] = jnp.where(row < live, tiles[-1], NEG)
    if shifted:
        top = functools.reduce(jnp.maximum, [jnp.max(t, axis=0, keepdims=True) for t in tiles])
        tiles = [t - top for t in tiles]
    expd = [jnp.exp(t) for t in tiles]
    total = functools.reduce(jnp.add, [jnp.sum(t, axis=0, keepdims=True) for t in expd])
    inv = 1.0 / total
    return [t * inv for t in expd]


def attend_kernel(
    groups, blk, hw, head_dim, at_ref, x_ref, out_ref, kv, qs, res, kvt, pb
):
    heads = hw // head_dim
    scale = 1.0 / math.sqrt(head_dim)
    rows = out_ref.shape[1] * 2
    half = rows // 2
    per_group = rows // blk
    total = groups * rows

    kv[pl.ds(total, KT), :] = jnp.zeros((KT, 2 * hw), BF16)
    qs[pl.ds(total, KT), :] = jnp.zeros((KT, 2 * hw), BF16)
    qs[0:total, hw:2 * hw] = jnp.zeros((total, hw), BF16)

    for side in range(2):
        def place(b, g, r):
            to = pl.multiple_of(at_ref[0, b] * blk, blk)
            kv[pl.ds(to, blk), :] = x_ref[g, pl.ds(r, blk), :]
            from_row = pl.multiple_of(r + (rows - side * half), blk)
            qs[pl.ds(to, blk), 0:hw] = x_ref[g, pl.ds(from_row, blk), side * hw:(side + 1) * hw]

        each_block(groups, per_group, blk, place, side * per_group // 2, per_group // 2)

    key_norm = largest_norm([kv[t:t + rows, :] for t in range(0, total, rows)], hw, head_dim)
    query_norm = largest_norm([qs[t:t + rows, :] for t in range(0, total, rows)], hw, head_dim)
    small = key_norm * query_norm * (scale * scale) < 2500.0

    def patch(slots, base, live, shifted):
        kvt[:, 0:slots] = kv[pl.ds(base, slots), :].T
        pb[0:slots, :] = jnp.zeros((slots, heads * QT), BF16)

        def flush(c):
            at = pl.multiple_of(base + c * QT, blk)
            wide = dot(kvt[hw:2 * hw, 0:slots], pb[0:slots, :])
            res[pl.ds(at, QT), :] = own_blocks(wide, head_dim, heads).astype(BF16)

        def chunk(c, carry):
            at = pl.multiple_of(base + c * QT, blk)
            q = (qs[pl.ds(at, QT), :].astype(F32) * scale).astype(BF16)
            q_st = stacked(q, head_dim, heads, 0)
            scores = [
                dot(kv[pl.ds(pl.multiple_of(base + t, blk), KT), :], q_st, NT)
                for t in range(0, slots, KT)
            ]
            flush(jnp.maximum(c - 1, 0))
            for t, p in enumerate(probs_of(scores, live, shifted)):
                pb[t * KT:(t + 1) * KT, :] = p.astype(BF16)
            return carry

        chunks = (live + QT - 1) // QT
        lax.fori_loop(0, chunks, chunk, 0)
        flush(chunks - 1)

    each_patch(0, groups, blk, at_ref, small, patch)

    for side in range(2):
        def back(b, g, r):
            at = pl.multiple_of(at_ref[0, b] * blk, blk)
            to = pl.multiple_of(r - side * half, blk)
            out_ref[g, pl.ds(to, blk), side * hw:(side + 1) * hw] = res[pl.ds(at, blk), :]

        each_block(groups, per_group, blk, back, side * per_group // 2, per_group // 2)


def attend_grad_kernel(
    groups, blk, hw, head_dim, at_ref, x_ref, out_ref, kv, qd, dq, dkv, kvt, both, acc, right
):
    heads = hw // head_dim
    scale = 1.0 / math.sqrt(head_dim)
    rows = out_ref.shape[1] * 2 // 3
    half = rows // 2
    per_group = rows // blk
    total = groups * rows
    span = heads * QT

    kv[pl.ds(total, KT), :] = jnp.zeros((KT, 2 * hw), BF16)
    qd[pl.ds(total, KT), :] = jnp.zeros((KT, 2 * hw), BF16)

    def place(b, g, r):
        to = pl.multiple_of(at_ref[1, b] * blk, blk)
        kv[pl.ds(to, blk), :] = x_ref[g, pl.ds(r, blk), :]
        qd[pl.ds(to, blk), :] = x_ref[g, pl.ds(pl.multiple_of(r + rows, blk), blk), :]

    each_block(groups, per_group, blk, place)

    key_norm = largest_norm([kv[t:t + rows, :] for t in range(0, total, rows)], hw, head_dim)
    query_norm = largest_norm([qd[t:t + rows, :] for t in range(0, total, rows)], hw, head_dim)
    small = key_norm * query_norm * (scale * scale) < 2500.0

    def patch(slots, base, live, shifted):
        kvt[:, 0:slots] = kv[pl.ds(base, slots), :].T
        acc[0:slots, :] = jnp.zeros((slots, 2 * hw), F32)
        both[0:slots, :] = jnp.zeros((slots, 2 * span), BF16)
        right[...] = jnp.zeros(right.shape, BF16)

        def flush(c):
            at = pl.multiple_of(base + c * QT, blk)
            acc[0:slots, :] += dot(both[0:slots, :], right[...])
            wide = dot(kvt[0:hw, 0:slots], both[0:slots, 0:span]) * scale
            dq[pl.ds(at, QT), :] = own_blocks(wide, head_dim, heads).astype(BF16)

        def chunk(c, carry):
            at = pl.multiple_of(base + c * QT, blk)
            tile = qd[pl.ds(at, QT), :]
            q_st = stacked((tile.astype(F32) * scale).astype(BF16), head_dim, heads, 0)
            row = lax.broadcasted_iota(jnp.int32, tile.shape, 0) + c * QT
            d_st = stacked(jnp.where(row < live, tile, jnp.zeros_like(tile)), head_dim, heads, hw)
            keys = [
                kv[pl.ds(pl.multiple_of(base + t, blk), KT), :] for t in range(0, slots, KT)
            ]
            scores = [dot(k, q_st, NT) for k in keys]
            grads = [dot(k, d_st, NT) for k in keys]
            flush(jnp.maximum(c - 1, 0))
            right[0:span, :] = q_st
            right[span:2 * span, :] = d_st
            probs = probs_of(scores, live, shifted)
            delta = functools.reduce(
                jnp.add, [jnp.sum(p * g, axis=0, keepdims=True) for p, g in zip(probs, grads)]
            )
            for t, (p, g) in enumerate(zip(probs, grads)):
                both[t * KT:(t + 1) * KT, 0:span] = (p * (g - delta)).astype(BF16)
                both[t * KT:(t + 1) * KT, span:2 * span] = p.astype(BF16)
            return carry

        chunks = (live + QT - 1) // QT
        lax.fori_loop(0, chunks, chunk, 0)
        flush(chunks - 1)
        dkv[pl.ds(base, slots), :] = acc[0:slots, :].astype(BF16)

    each_patch(1, groups, blk, at_ref, small, patch)

    for side in range(2):
        def back(b, g, r):
            at = pl.multiple_of(at_ref[1, b] * blk, blk)
            out_ref[g, pl.ds(r, blk), :] = dkv[pl.ds(at, blk), :]
            to = pl.multiple_of(r + (rows - side * half), blk)
            out_ref[g, pl.ds(to, blk), side * hw:(side + 1) * hw] = dq[pl.ds(at, blk), :]

        each_block(groups, per_group, blk, back, side * per_group // 2, per_group // 2)


def mix_kernel(groups, hw, att_ref, rows_ref, wproj_ref, out_ref, a_ref):
    half = a_ref.shape[0] // 2
    for g in range(groups):
        a_ref[0:half, g * hw:(g + 1) * hw] = att_ref[g, :, 0:hw]
        a_ref[half:2 * half, g * hw:(g + 1) * hw] = att_ref[g, :, hw:2 * hw]
    mixed = rows_ref[...].astype(F32) + dot(a_ref[...], wproj_ref[...])
    out_ref[...] = mixed.astype(BF16)


def input_grad_kernel(
    groups, hw, pick_ref, dqkv_ref, rows_ref, up_ref, gain_ref, wqkv_ref, out_ref, y_ref
):
    rows, width = up_ref.shape
    half = rows // 2
    for g in range(groups):
        low = g * hw
        y_ref[:, width + low:width + low + hw] = dqkv_ref[g, 0:rows, 0:hw]
        y_ref[:, 2 * width + low:2 * width + low + hw] = dqkv_ref[g, 0:rows, hw:2 * hw]
        y_ref[0:half, low:low + hw] = dqkv_ref[g, rows:rows + half, 0:hw]
        y_ref[half:rows, low:low + hw] = dqkv_ref[g, rows:rows + half, hw:2 * hw]
    grad = dot(y_ref[...], wqkv_ref[...], NT) * gain_ref[...]
    center, inv = centered(rows_ref[0].astype(F32))
    unit = center * inv
    mean = jnp.mean(grad, axis=-1, keepdims=True)
    along = jnp.mean(grad * unit, axis=-1, keepdims=True)
    pulled = inv * (grad - mean - unit * along)
    out_ref[...] = (up_ref[...].astype(F32) + pulled).astype(BF16)


def call(kernel, out_shape, operands, scratch=(), smem=0, cost=None, name=None, picked=None):
    specs = [pl.BlockSpec(memory_space=pltpu.SMEM)] * smem
    specs += [pl.BlockSpec(memory_space=pltpu.VMEM)] * (len(operands) - smem)
    kwargs = dict(
        out_shape=jax.ShapeDtypeStruct(out_shape, BF16),
        cost_estimate=pl.CostEstimate(flops=cost[0], bytes_accessed=cost[1], transcendentals=0),
        compiler_params=pltpu.CompilerParams(vmem_limit_bytes=VMEM_LIMIT),
        name=name,
    )
    if picked is None:
        return pl.pallas_call(
            kernel,
            in_specs=specs,
            out_specs=pl.BlockSpec(memory_space=pltpu.VMEM),
            scratch_shapes=list(scratch),
            **kwargs,
        )(*operands)

    def whole(shape):
        return pl.BlockSpec(shape, lambda i, pick: (0,) * len(shape))

    specs = [whole(o.shape) for o in operands[1:]]
    stash = operands[picked]
    specs[picked - 1] = pl.BlockSpec((1,) + stash.shape[1:], lambda i, pick: (pick[0], 0, 0))
    return pl.pallas_call(
        kernel,
        grid_spec=pltpu.PrefetchScalarGridSpec(
            num_scalar_prefetch=1,
            grid=(1,),
            in_specs=specs,
            out_specs=whole(out_shape),
            scratch_shapes=list(scratch),
        ),
        **kwargs,
    )(*operands)


def places(owners, groups):
    count = owners.shape[1]
    key = owners * count + jnp.arange(count, dtype=jnp.int32)
    bounds = jnp.broadcast_to(jnp.arange(groups + 1, dtype=jnp.int32) * count, (2, groups + 1))
    marks = jnp.concatenate([key, bounds], axis=1)
    return jnp.sum((key[:, None, :] < marks[:, :, None]).astype(jnp.int32), axis=2)


def swap(value):
    return lax.all_to_all(value, "space", split_axis=0, concat_axis=0, tiled=True)


def on_device(
    act_in, stash, plan, grad_in, fwd_owner, stash_owner, ln_gain, qkv_weight, proj_weight
):
    groups = lax.axis_size("space")
    rows_in = act_in[0]
    rows, width = rows_in.shape
    head_dim = width // HEADS
    hw = width // groups
    blk = rows // groups
    heads = hw // head_dim
    total = groups * rows
    span = heads * QT
    w_qkv = qkv_weight[0]
    w_proj = proj_weight[0]
    stored = stash[0]
    upstream = grad_in[0]
    stored_owners = lax.dynamic_index_in_dim(stash_owner[0], plan[0], 0, keepdims=False)
    mine = jnp.stack([fwd_owner[0], stored_owners]).reshape(2, groups, blk)[:, :, 0]
    owner_rows = jnp.pad(mine.astype(BF16), ((0, 14), (0, 2 * hw - groups)))

    sent_b = call(
        functools.partial(project_grad_kernel, groups, hw),
        (groups, 2 * rows + 16, 2 * hw),
        (plan, stored, upstream, ln_gain, w_qkv, w_proj, owner_rows),
        [pltpu.VMEM((rows, 3 * width), BF16), pltpu.VMEM((rows, width), BF16)],
        cost=(8 * rows * width * width, 6 * 1024 * 1024),
        name="project_grad",
        picked=1,
    )
    got_b = swap(sent_b)
    sent = call(
        functools.partial(project_kernel, groups, hw),
        (groups, 3 * rows // 2, 2 * hw),
        (rows_in, ln_gain, w_qkv),
        [pltpu.VMEM((rows, 3 * width), BF16)],
        cost=(6 * rows * width * width, 5 * 1024 * 1024),
        name="project",
    )
    got = swap(sent)
    owners = got_b[:, 2 * rows:2 * rows + 2, 0:groups].astype(jnp.int32)
    at = places(owners.transpose(1, 0, 2).reshape(2, groups * groups), groups)
    grads = call(
        functools.partial(attend_grad_kernel, groups, blk, hw, head_dim),
        (groups, 3 * rows // 2, 2 * hw),
        (at, got_b),
        [
            pltpu.VMEM((total + KT, 2 * hw), BF16),
            pltpu.VMEM((total + KT, 2 * hw), BF16),
            pltpu.VMEM((total + KT, hw), BF16),
            pltpu.VMEM((total + KT, 2 * hw), BF16),
            pltpu.VMEM((2 * hw, PATCH), BF16),
            pltpu.VMEM((PATCH, 2 * span), BF16),
            pltpu.VMEM((PATCH, 2 * hw), F32),
            pltpu.VMEM((2 * span, 2 * hw), BF16),
        ],
        smem=1,
        cost=(30_000_000_000, 4 * 1024 * 1024),
        name="attend_grad",
    )
    grads, got = lax.optimization_barrier((grads, got))
    ret_grads = swap(grads)
    attended = call(
        functools.partial(attend_kernel, groups, blk, hw, head_dim),
        (groups, rows // 2, 2 * hw),
        (at, got),
        [
            pltpu.VMEM((total + KT, 2 * hw), BF16),
            pltpu.VMEM((total + KT, 2 * hw), BF16),
            pltpu.VMEM((total + KT, hw), BF16),
            pltpu.VMEM((2 * hw, PATCH), BF16),
            pltpu.VMEM((PATCH, span), BF16),
        ],
        smem=1,
        cost=(20_000_000_000, 3 * 1024 * 1024),
        name="attend",
    )
    ret_grads, attended = lax.optimization_barrier((ret_grads, attended))
    ret = swap(attended)
    input_grad = call(
        functools.partial(input_grad_kernel, groups, hw),
        (rows, width),
        (plan, ret_grads, stored, upstream, ln_gain, w_qkv),
        [pltpu.VMEM((rows, 3 * width), BF16)],
        cost=(6 * rows * width * width, 5 * 1024 * 1024),
        name="input_grad",
        picked=2,
    )
    grad_out = passed_along(input_grad[None], "section", -1)
    mixed = call(
        functools.partial(mix_kernel, groups, hw),
        (rows, width),
        (ret, rows_in, w_proj),
        [pltpu.VMEM((rows, width), BF16)],
        cost=(2 * rows * width * width, 2 * 1024 * 1024),
        name="mix",
    )
    act_out = passed_along(mixed[None], "section", 1)
    return (act_out, grad_out)


def solution(mesh):
    in_specs = (
        P("section", "space", None),
        P("section", None, "space", None),
        P("section"),
        P("section", "space", None),
        P("section", "space"),
        P("section", None, "space"),
        P("section", None),
        P("section", None, None),
        P("section", None, None),
    )
    out_specs = (P("section", "space", None), P("section", "space", None))
    return jax.shard_map(
        on_device, mesh=mesh, in_specs=in_specs, out_specs=out_specs, check_vma=False
    )
```

time: 220 us -> 190 us (0.86)
  blocking collectives: 19.8 us -> 0 us
  local copies, waits for them, and re-layouts: 18.9 us -> 3.31 us
  Pallas kernels: 128 us -> 117 us
  starting transfers between devices: 23.4 us -> 33.6 us
  waiting for transfers between devices: 27.5 us -> 32.8 us
    all_gather x1 -> x0, blocking collectives: 19.8 us -> none  [on_device(): owners = lax.all_gather(mine, 'space', axis=0)]
    ppermute x2, starting transfers between devices: 3.82 us -> 15.3 us  [passed_along(): return lax.ppermute(value, axis, pairs)]
    pallas_call x4, Pallas kernels: 118 us -> 107 us  [call(): pl.pallas_call(kernel, in_specs=specs, out_specs=pl.BlockSpec(memory_spac...]
    pallas_call x3 -> x0, local copies, waits for them, and re-layouts: 10.1 us -> none  [call(): pl.pallas_call(kernel, in_specs=specs, out_specs=pl.BlockSpec(memory_spac...]
    all_to_all x4, waiting for transfers between devices: 13.4 us -> 21.1 us  [swap(): lax.all_to_all(value, 'space', split_axis=0, concat_axis=0, tiled=True)]
    all_to_all x3 -> x0, local copies, waits for them, and re-layouts: 6.15 us -> none  [swap(): lax.all_to_all(value, 'space', split_axis=0, concat_axis=0, tiled=True)]
    ppermute x2, waiting for transfers between devices: 14.1 us -> 11.7 us  [passed_along(): return lax.ppermute(value, axis, pairs)]
  transfers between devices with their start and end apart: 6 -> 6, of which waited for: 2 -> 3; matrix products, arithmetic and copies ran while one was open for 7% -> 0% of each run, Pallas kernels for 56% -> 59%
where the time goes in v2:
time: 190 us
  Pallas kernels  117 us (62%)
  starting transfers between devices  33.6 us (18%)
  waiting for transfers between devices  32.8 us (17%)
  local copies, waits for them, and re-layouts  3.31 us (2%)
  other arithmetic  2.2 us (1%)
    pallas_call x4, Pallas kernels, call(): pl.pallas_call(kernel, in_specs=specs, out_specs=pl.BlockSpec(memory_spac...  107 us
    all_to_all x4, waiting for transfers between devices, swap(): lax.all_to_all(value, 'space', split_axis=0, concat_axis=0, tiled=True)  21.1 us
    all_to_all x4, starting transfers between devices, swap(): lax.all_to_all(value, 'space', split_axis=0, concat_axis=0, tiled=True)  18.4 us
    ppermute x2, starting transfers between devices, passed_along(): return lax.ppermute(value, axis, pairs)  15.3 us
    ppermute x2, waiting for transfers between devices, passed_along(): return lax.ppermute(value, axis, pairs)  11.7 us
    pallas_call x2, Pallas kernels, call(): pl.pallas_call(kernel, grid_spec=pltpu.PrefetchScalarGridSpec(num_scalar_...  9.97 us
  transfers between devices with their start and end apart: 6, of which 3 were waited for; matrix products, arithmetic and copies ran while one was open for 0% of the time, Pallas kernels for 59%

profile of v2, /device:TPU:10, one launch (start us, length us, event | category | flops | bytes accessed | tf_op | source)
XLA Modules:
  0.0 190.2 jit_solution(8888191301022282178)
XLA Ops:
  1.3 0.7 convert_reduce_fusion.1
  2.0 0.1 stack.9
  2.1 0.7 convert_reduce_fusion.2
  2.8 0.1 stack.8
  2.9 0.1 fusion
  3.0 0.6 pad.4.owners_ref
  3.6 5.2 %project_grad.1 = bf16[8,1040,128]{2,1,0:T(8,128)(2,1)} custom-call(s32[1]{0:T(128)} %copy.19.pick_ref, bf16[4,512,512]{2,1,0:T(8,128)(2,1)} %bitcast.16, bf16[512,512]{1,0:T(8,128)(2,1)} %bitcast.18, f32[1,512]{1,0:T(1,128)} %gain_ref.5, bf16[512,1536]{1,0:T(8,128)(2,1)} %bitcast.13, bf16[512,512]{1,0:T(8,128)(2,1)} %bitcast.20, bf16[16,128]{1,0:T(8,128)(2,1)} %pad.4.owners_ref), custom_call_target="tpu_custom_call" | custom-call | flops 1073741824 | bytes 6291456 | tf_op jit(solution)/shard_map/project_grad/pallas_call | solution.py:358
  8.8 4.3 %all-to-all-start = ((bf16[8,1040,128]{2,1,0:T(8,128)(2,1)}), bf16[8,1040,128]{2,1,0:T(8,128)(2,1)S(1)}, u32[]{:S(2)}, u32[]{:S(2)}) async-start(bf16[8,1040,128]{2,1,0:T(8,128)(2,1)} %project_grad.1), calls=%async_computation | async-start | bytes 4259840 | tf_op jit(solution)/shard_map/all_to_all | solution.py:380
  13.0 0.1 pad.6.clone
  13.1 4.3 %project.1 = bf16[8,768,128]{2,1,0:T(8,128)(2,1)} custom-call(bf16[512,512]{1,0:T(8,128)(2,1)} %bitcast.22, f32[1,512]{1,0:T(1,128)} %gain_ref.5, bf16[512,1536]{1,0:T(8,128)(2,1)} %bitcast.14), custom_call_target="tpu_custom_call" | custom-call | flops 805306368 | bytes 5242880 | tf_op jit(solution)/shard_map/project/pallas_call | solution.py:344
  17.4 21.1 %all-to-all-done.x_ref = bf16[8,1040,128]{2,1,0:T(8,128)(2,1)S(1)} async-done(((bf16[8,1040,128]{2,1,0:T(8,128)(2,1)}), bf16[8,1040,128]{2,1,0:T(8,128)(2,1)S(1)}, u32[]{:S(2)}, u32[]{:S(2)}) %all-to-all-start) | async-done | bytes 2129952 | tf_op jit(solution)/shard_map/all_to_all | solution.py:380
  38.5 0.0 copy-start.1
  38.5 5.7 %all-to-all-start.1 = ((bf16[8,768,128]{2,1,0:T(8,128)(2,1)}), bf16[8,768,128]{2,1,0:T(8,128)(2,1)}, u32[]{:S(2)}, u32[]{:S(2)}) async-start(bf16[8,768,128]{2,1,0:T(8,128)(2,1)} %project.1), calls=%async_computation.1 | async-start | bytes 3145728 | tf_op jit(solution)/shard_map/all_to_all | solution.py:380
  44.2 0.0 copy-done.1
  44.2 0.1 mul.22
  44.3 0.7 convert_reduce_fusion.at_ref
  45.0 60.8 %attend_grad.1 = bf16[8,768,128]{2,1,0:T(8,128)(2,1)} custom-call(s32[2,73]{1,0:T(2,128)} %convert_reduce_fusion.at_ref, bf16[8,1040,128]{2,1,0:T(8,128)(2,1)} %copy-done.1), custom_call_target="tpu_custom_call" | custom-call | flops 30000001024 | bytes 4194304 | tf_op jit(solution)/shard_map/attend_grad/pallas_call | solution.py:344
  105.7 0.0 all-to-all-done.1.x_ref
  105.7 4.2 %all-to-all-start.2 = ((bf16[8,768,128]{2,1,0:T(8,128)(2,1)}), bf16[8,768,128]{2,1,0:T(8,128)(2,1)S(1)}, u32[]{:S(2)}, u32[]{:S(2)}) async-start(bf16[8,768,128]{2,1,0:T(8,128)(2,1)} %attend_grad.1), calls=%async_computation.2 | async-start | bytes 3145728 | tf_op jit(solution)/shard_map/all_to_all | solution.py:380
  110.0 39.2 %attend.1 = bf16[8,256,128]{2,1,0:T(8,128)(2,1)} custom-call(s32[2,73]{1,0:T(2,128)} %convert_reduce_fusion.at_ref, bf16[8,768,128]{2,1,0:T(8,128)(2,1)} %all-to-all-done.1.x_ref), custom_call_target="tpu_custom_call" | custom-call | flops 20000000000 | bytes 3145728 | tf_op jit(solution)/shard_map/attend/pallas_call | solution.py:344
  149.1 0.0 all-to-all-done.2.dqkv_ref
  149.1 0.0 copy-start
  149.1 4.2 %all-to-all-start.3 = ((bf16[8,256,128]{2,1,0:T(8,128)(2,1)}), bf16[8,256,128]{2,1,0:T(8,128)(2,1)S(1)}, u32[]{:S(2)}, u32[]{:S(2)}) async-start(bf16[8,256,128]{2,1,0:T(8,128)(2,1)} %attend.1), calls=%async_computation.3 | async-start | bytes 1048576 | tf_op jit(solution)/shard_map/all_to_all | solution.py:380
  153.3 0.0 copy-done
  153.3 4.8 %input_grad.1 = bf16[512,512]{1,0:T(8,128)(2,1)} custom-call(s32[1]{0:T(128)} %copy.19.pick_ref, bf16[8,768,128]{2,1,0:T(8,128)(2,1)} %copy-done, bf16[4,512,512]{2,1,0:T(8,128)(2,1)} %bitcast.17, bf16[512,512]{1,0:T(8,128)(2,1)} %bitcast.19, f32[1,512]{1,0:T(1,128)} %gain_ref.5, bf16[512,1536]{1,0:T(8,128)(2,1)} %bitcast.15), custom_call_target="tpu_custom_call" | custom-call | flops 805306368 | bytes 5242880 | tf_op jit(solution)/shard_map/input_grad/pallas_call | solution.py:358
  158.1 6.8 %collective-permute-start.1 = (bf16[1,512,512]{2,1,0:T(8,128)(2,1)}, bf16[1,512,512]{2,1,0:T(8,128)(2,1)S(1)}, u32[]{:S(2)}, u32[]{:S(2)}) collective-permute-start(bf16[1,512,512]{2,1,0:T(8,128)(2,1)} %bitcast.24), channel_id=1, source_target_pairs={{8,0},{16,8},{24,16},{9,1},{17,9},{25,17},{10,2},{18,10},{26,18},{... | collective-permute-start | bytes 1572872 | tf_op jit(solution)/shard_map/ppermute | solution.py:31
  164.9 0.0 all-to-all-done.3.att_ref
  164.9 0.0 copy-start.2
  164.9 0.8 copy-done.2
  165.7 2.7 %mix.1 = bf16[512,512]{1,0:T(8,128)(2,1)} custom-call(bf16[8,256,128]{2,1,0:T(8,128)(2,1)} %copy-done.2, bf16[512,512]{1,0:T(8,128)(2,1)} %bitcast.23, bf16[512,512]{1,0:T(8,128)(2,1)} %bitcast.21), custom_call_target="tpu_custom_call" | custom-call | flops 268435456 | bytes 2097152 | tf_op jit(solution)/shard_map/mix/pallas_call | solution.py:344
  168.4 8.5 %collective-permute-start = (bf16[1,512,512]{2,1,0:T(8,128)(2,1)}, bf16[1,512,512]{2,1,0:T(8,128)(2,1)S(1)}, u32[]{:S(2)}, u32[]{:S(2)}) collective-permute-start(bf16[1,512,512]{2,1,0:T(8,128)(2,1)} %bitcast.25), channel_id=1, source_target_pairs={{0,8},{8,16},{16,24},{1,9},{9,17},{17,25},{2,10},{10,18},{18,26},{... | collective-permute-start | bytes 1572872 | tf_op jit(solution)/shard_map/ppermute | solution.py:31
  177.0 5.4 %collective-permute-done.1 = bf16[1,512,512]{2,1,0:T(8,128)(2,1)S(1)} collective-permute-done((bf16[1,512,512]{2,1,0:T(8,128)(2,1)}, bf16[1,512,512]{2,1,0:T(8,128)(2,1)S(1)}, u32[]{:S(2)}, u32[]{:S(2)}) %collective-permute-start.1) | collective-permute-done | bytes 524320 | tf_op jit(solution)/shard_map/ppermute | solution.py:31
  182.4 6.3 %collective-permute-done = bf16[1,512,512]{2,1,0:T(8,128)(2,1)S(1)} collective-permute-done((bf16[1,512,512]{2,1,0:T(8,128)(2,1)}, bf16[1,512,512]{2,1,0:T(8,128)(2,1)S(1)}, u32[]{:S(2)}, u32[]{:S(2)}) %collective-permute-start) | collective-permute-done | bytes 524320 | tf_op jit(solution)/shard_map/ppermute | solution.py:31
  188.7 0.8 copy.20
  189.5 0.8 copy.21
  (5 shorter events, 0.0 us)
Async XLA Ops:
  8.8 29.7 %all-to-all-start = ((bf16[8,1040,128]{2,1,0:T(8,128)(2,1)}), bf16[8,1040,128]{2,1,0:T(8,128)(2,1)S(1)}, u32[]{:S(2)}, u32[]{:S(2)}) async-start(bf16[8,1040,128]{2,1,0:T(8,128)(2,1)} %project_grad.1), calls=%async_computation | async-start | bytes 4259840 | tf_op jit(solution)/shard_map/all_to_all | solution.py:380
  38.5 5.7 %copy-start.1 = (bf16[8,1040,128]{2,1,0:T(8,128)(2,1)}, bf16[8,1040,128]{2,1,0:T(8,128)(2,1)S(1)}, u32[]{:S(2)}) copy-start(bf16[8,1040,128]{2,1,0:T(8,128)(2,1)S(1)} %all-to-all-done.x_ref) | copy-start | bytes 6389764
  38.5 67.2 %all-to-all-start.1 = ((bf16[8,768,128]{2,1,0:T(8,128)(2,1)}), bf16[8,768,128]{2,1,0:T(8,128)(2,1)}, u32[]{:S(2)}, u32[]{:S(2)}) async-start(bf16[8,768,128]{2,1,0:T(8,128)(2,1)} %project.1), calls=%async_computation.1 | async-start | bytes 3145728 | tf_op jit(solution)/shard_map/all_to_all | solution.py:380
  105.7 43.4 %all-to-all-start.2 = ((bf16[8,768,128]{2,1,0:T(8,128)(2,1)}), bf16[8,768,128]{2,1,0:T(8,128)(2,1)S(1)}, u32[]{:S(2)}, u32[]{:S(2)}) async-start(bf16[8,768,128]{2,1,0:T(8,128)(2,1)} %attend_grad.1), calls=%async_computation.2 | async-start | bytes 3145728 | tf_op jit(solution)/shard_map/all_to_all | solution.py:380
  149.1 4.2 %copy-start = (bf16[8,768,128]{2,1,0:T(8,128)(2,1)}, bf16[8,768,128]{2,1,0:T(8,128)(2,1)S(1)}, u32[]{:S(2)}) copy-start(bf16[8,768,128]{2,1,0:T(8,128)(2,1)S(1)} %all-to-all-done.2.dqkv_ref) | copy-start | bytes 4718596
  149.1 15.8 %all-to-all-start.3 = ((bf16[8,256,128]{2,1,0:T(8,128)(2,1)}), bf16[8,256,128]{2,1,0:T(8,128)(2,1)S(1)}, u32[]{:S(2)}, u32[]{:S(2)}) async-start(bf16[8,256,128]{2,1,0:T(8,128)(2,1)} %attend.1), calls=%async_computation.3 | async-start | bytes 1048576 | tf_op jit(solution)/shard_map/all_to_all | solution.py:380
  158.1 24.2 %collective-permute-start.1 = (bf16[1,512,512]{2,1,0:T(8,128)(2,1)}, bf16[1,512,512]{2,1,0:T(8,128)(2,1)S(1)}, u32[]{:S(2)}, u32[]{:S(2)}) collective-permute-start(bf16[1,512,512]{2,1,0:T(8,128)(2,1)} %bitcast.24), channel_id=1, source_target_pairs={{8,0},{16,8},{24,16},{9,1},{17,9},{25,17},{10,2},{18,10},{26,18},{... | collective-permute-start | bytes 1572872 | tf_op jit(solution)/shard_map/ppermute | solution.py:31
  164.9 0.8 copy-start.2
  168.4 20.2 %collective-permute-start = (bf16[1,512,512]{2,1,0:T(8,128)(2,1)}, bf16[1,512,512]{2,1,0:T(8,128)(2,1)S(1)}, u32[]{:S(2)}, u32[]{:S(2)}) collective-permute-start(bf16[1,512,512]{2,1,0:T(8,128)(2,1)} %bitcast.25), channel_id=1, source_target_pairs={{0,8},{8,16},{16,24},{1,9},{9,17},{17,25},{2,10},{10,18},{18,26},{... | collective-permute-start | bytes 1572872 | tf_op jit(solution)/shard_map/ppermute | solution.py:31

commit v3 on v2

--- a/solution.py
+++ b/solution.py
@@ -93,6 +93,15 @@
     return jnp.concatenate(parts, axis=0)
 
 
+def stacked_columns(tile_t, head_dim, heads, offset):
+    row = lax.broadcasted_iota(jnp.int32, tile_t.shape, 0)
+    parts = []
+    for h in range(heads):
+        low = offset + h * head_dim
+        parts.append(jnp.where((row >= low) & (row < low + head_dim), tile_t, 0.0))
+    return jnp.concatenate(parts, axis=1).astype(BF16)
+
+
 def own_blocks(wide, head_dim, heads):
     picked = [
         wide[h * head_dim:(h + 1) * head_dim, h * QT:(h + 1) * QT] for h in range(heads)
@@ -103,12 +112,12 @@
 def each_block(groups, per_group, blk, body, first=0, count=None):
     count = per_group if count is None else count
 
-    def step(b, carry):
-        g, j = b // count, first + b % count
-        body(g * per_group + j, g, pl.multiple_of(j * blk, blk))
+    def step(g, carry):
+        for j in range(first, first + count):
+            body(g * per_group + j, g, j * blk)
         return carry
 
-    lax.fori_loop(0, groups * count, step, 0)
+    lax.fori_loop(0, groups, step, 0)
 
 
 def each_patch(which, groups, blk, at_ref, small, body):
@@ -179,7 +188,7 @@
         def place(b, g, r):
             to = pl.multiple_of(at_ref[0, b] * blk, blk)
             kv[pl.ds(to, blk), :] = x_ref[g, pl.ds(r, blk), :]
-            from_row = pl.multiple_of(r + (rows - side * half), blk)
+            from_row = r + rows - side * half
             qs[pl.ds(to, blk), 0:hw] = x_ref[g, pl.ds(from_row, blk), side * hw:(side + 1) * hw]
 
         each_block(groups, per_group, blk, place, side * per_group // 2, per_group // 2)
@@ -199,10 +208,10 @@
 
         def chunk(c, carry):
             at = pl.multiple_of(base + c * QT, blk)
-            q = (qs[pl.ds(at, QT), :].astype(F32) * scale).astype(BF16)
-            q_st = stacked(q, head_dim, heads, 0)
+            q = qs[pl.ds(at, QT), :].astype(F32) * scale
+            q_cols = stacked_columns(q.T, head_dim, heads, 0)
             scores = [
-                dot(kv[pl.ds(pl.multiple_of(base + t, blk), KT), :], q_st, NT)
+                dot(kv[pl.ds(pl.multiple_of(base + t, blk), KT), :], q_cols)
                 for t in range(0, slots, KT)
             ]
             flush(jnp.maximum(c - 1, 0))
@@ -219,7 +228,7 @@
     for side in range(2):
         def back(b, g, r):
             at = pl.multiple_of(at_ref[0, b] * blk, blk)
-            to = pl.multiple_of(r - side * half, blk)
+            to = r - side * half
             out_ref[g, pl.ds(to, blk), side * hw:(side + 1) * hw] = res[pl.ds(at, blk), :]
 
         each_block(groups, per_group, blk, back, side * per_group // 2, per_group // 2)
@@ -242,7 +251,7 @@
     def place(b, g, r):
         to = pl.multiple_of(at_ref[1, b] * blk, blk)
         kv[pl.ds(to, blk), :] = x_ref[g, pl.ds(r, blk), :]
-        qd[pl.ds(to, blk), :] = x_ref[g, pl.ds(pl.multiple_of(r + rows, blk), blk), :]
+        qd[pl.ds(to, blk), :] = x_ref[g, pl.ds(r + rows, blk), :]
 
     each_block(groups, per_group, blk, place)
 
@@ -267,12 +276,16 @@
             tile = qd[pl.ds(at, QT), :]
             q_st = stacked((tile.astype(F32) * scale).astype(BF16), head_dim, heads, 0)
             row = lax.broadcasted_iota(jnp.int32, tile.shape, 0) + c * QT
-            d_st = stacked(jnp.where(row < live, tile, jnp.zeros_like(tile)), head_dim, heads, hw)
+            tile = jnp.where(row < live, tile, jnp.zeros_like(tile))
+            d_st = stacked(tile, head_dim, heads, hw)
+            tile_t = tile.astype(F32).T
+            q_cols = stacked_columns(tile_t * scale, head_dim, heads, 0)
+            d_cols = stacked_columns(tile_t, head_dim, heads, hw)
             keys = [
                 kv[pl.ds(pl.multiple_of(base + t, blk), KT), :] for t in range(0, slots, KT)
             ]
-            scores = [dot(k, q_st, NT) for k in keys]
-            grads = [dot(k, d_st, NT) for k in keys]
+            scores = [dot(k, q_cols) for k in keys]
+            grads = [dot(k, d_cols) for k in keys]
             flush(jnp.maximum(c - 1, 0))
             right[0:span, :] = q_st
             right[span:2 * span, :] = d_st
@@ -296,7 +309,7 @@
         def back(b, g, r):
             at = pl.multiple_of(at_ref[1, b] * blk, blk)
             out_ref[g, pl.ds(r, blk), :] = dkv[pl.ds(at, blk), :]
-            to = pl.multiple_of(r + (rows - side * half), blk)
+            to = r + rows - side * half
             out_ref[g, pl.ds(to, blk), side * hw:(side + 1) * hw] = dq[pl.ds(at, blk), :]
 
         each_block(groups, per_group, blk, back, side * per_group // 2, per_group // 2)

time: 190 us -> 187 us (0.984)
  starting transfers between devices: 33.6 us -> 24.4 us
  Pallas kernels: 117 us -> 120 us
  waiting for transfers between devices: 32.8 us -> 35 us
    ppermute x2, starting transfers between devices: 15.3 us -> 6.06 us  [passed_along(): return lax.ppermute(value, axis, pairs)]
    pallas_call x4, Pallas kernels: 107 us -> 110 us  [call(): pl.pallas_call(kernel, in_specs=specs, out_specs=pl.BlockSpec(memory_spac...]
    ppermute x2, waiting for transfers between devices: 11.7 us -> 13.9 us  [passed_along(): return lax.ppermute(value, axis, pairs)]
  transfers between devices with their start and end apart: 6 -> 6, of which waited for: 3 -> 3; matrix products, arithmetic and copies ran while one was open for 0% -> 0% of each run, Pallas kernels for 59% -> 62%
where the time goes in v3:
time: 187 us; the launch traced here: 186 us
  Pallas kernels  120 us (64%)
  waiting for transfers between devices  35 us (19%)
  starting transfers between devices  24.4 us (13%)
  local copies, waits for them, and re-layouts  3.32 us (2%)
  other arithmetic  2.2 us (1%)
    pallas_call x4, Pallas kernels, call(): pl.pallas_call(kernel, in_specs=specs, out_specs=pl.BlockSpec(memory_spac...  110 us
    all_to_all x4, waiting for transfers between devices, swap(): lax.all_to_all(value, 'space', split_axis=0, concat_axis=0, tiled=True)  21.1 us
    all_to_all x4, starting transfers between devices, swap(): lax.all_to_all(value, 'space', split_axis=0, concat_axis=0, tiled=True)  18.4 us
    ppermute x2, waiting for transfers between devices, passed_along(): return lax.ppermute(value, axis, pairs)  13.9 us
    pallas_call x2, Pallas kernels, call(): pl.pallas_call(kernel, grid_spec=pltpu.PrefetchScalarGridSpec(num_scalar_...  9.97 us
    ppermute x2, starting transfers between devices, passed_along(): return lax.ppermute(value, axis, pairs)  6.06 us
  transfers between devices with their start and end apart: 6, of which 3 were waited for; matrix products, arithmetic and copies ran while one was open for 0% of the time, Pallas kernels for 62%

profile of v3, /device:TPU:10, one launch (start us, length us, event | category | flops | bytes accessed | tf_op | source)
XLA Modules:
  0.0 186.2 jit_solution(11119951934708300938)
XLA Ops:
  1.3 0.7 convert_reduce_fusion.1
  2.0 0.1 stack.9
  2.1 0.7 convert_reduce_fusion.2
  2.8 0.1 stack.8
  2.9 0.1 fusion
  3.0 0.6 pad.4.owners_ref
  3.6 5.2 %project_grad.1 = bf16[8,1040,128]{2,1,0:T(8,128)(2,1)} custom-call(s32[1]{0:T(128)} %copy.19.pick_ref, bf16[4,512,512]{2,1,0:T(8,128)(2,1)} %bitcast.16, bf16[512,512]{1,0:T(8,128)(2,1)} %bitcast.18, f32[1,512]{1,0:T(1,128)} %gain_ref.5, bf16[512,1536]{1,0:T(8,128)(2,1)} %bitcast.13, bf16[512,512]{1,0:T(8,128)(2,1)} %bitcast.20, bf16[16,128]{1,0:T(8,128)(2,1)} %pad.4.owners_ref), custom_call_target="tpu_custom_call" | custom-call | flops 1073741824 | bytes 6291456 | tf_op jit(solution)/shard_map/project_grad/pallas_call | solution.py:371
  8.8 4.3 %all-to-all-start = ((bf16[8,1040,128]{2,1,0:T(8,128)(2,1)}), bf16[8,1040,128]{2,1,0:T(8,128)(2,1)S(1)}, u32[]{:S(2)}, u32[]{:S(2)}) async-start(bf16[8,1040,128]{2,1,0:T(8,128)(2,1)} %project_grad.1), calls=%async_computation | async-start | bytes 4259840 | tf_op jit(solution)/shard_map/all_to_all | solution.py:393
  13.0 0.1 pad.6.clone
  13.1 4.3 %project.1 = bf16[8,768,128]{2,1,0:T(8,128)(2,1)} custom-call(bf16[512,512]{1,0:T(8,128)(2,1)} %bitcast.22, f32[1,512]{1,0:T(1,128)} %gain_ref.5, bf16[512,1536]{1,0:T(8,128)(2,1)} %bitcast.14), custom_call_target="tpu_custom_call" | custom-call | flops 805306368 | bytes 5242880 | tf_op jit(solution)/shard_map/project/pallas_call | solution.py:357
  17.4 21.1 %all-to-all-done.x_ref = bf16[8,1040,128]{2,1,0:T(8,128)(2,1)S(1)} async-done(((bf16[8,1040,128]{2,1,0:T(8,128)(2,1)}), bf16[8,1040,128]{2,1,0:T(8,128)(2,1)S(1)}, u32[]{:S(2)}, u32[]{:S(2)}) %all-to-all-start) | async-done | bytes 2129952 | tf_op jit(solution)/shard_map/all_to_all | solution.py:393
  38.5 0.0 copy-start.1
  38.5 5.7 %all-to-all-start.1 = ((bf16[8,768,128]{2,1,0:T(8,128)(2,1)}), bf16[8,768,128]{2,1,0:T(8,128)(2,1)}, u32[]{:S(2)}, u32[]{:S(2)}) async-start(bf16[8,768,128]{2,1,0:T(8,128)(2,1)} %project.1), calls=%async_computation.1 | async-start | bytes 3145728 | tf_op jit(solution)/shard_map/all_to_all | solution.py:393
  44.2 0.0 copy-done.1
  44.2 0.1 mul.22
  44.3 0.7 convert_reduce_fusion.at_ref
  45.0 66.9 %attend_grad.1 = bf16[8,768,128]{2,1,0:T(8,128)(2,1)} custom-call(s32[2,73]{1,0:T(2,128)} %convert_reduce_fusion.at_ref, bf16[8,1040,128]{2,1,0:T(8,128)(2,1)} %copy-done.1), custom_call_target="tpu_custom_call" | custom-call | flops 30000001024 | bytes 4194304 | tf_op jit(solution)/shard_map/attend_grad/pallas_call | solution.py:357
  111.9 0.0 all-to-all-done.1.x_ref
  111.9 4.2 %all-to-all-start.2 = ((bf16[8,768,128]{2,1,0:T(8,128)(2,1)}), bf16[8,768,128]{2,1,0:T(8,128)(2,1)S(1)}, u32[]{:S(2)}, u32[]{:S(2)}) async-start(bf16[8,768,128]{2,1,0:T(8,128)(2,1)} %attend_grad.1), calls=%async_computation.2 | async-start | bytes 3145728 | tf_op jit(solution)/shard_map/all_to_all | solution.py:393
  116.1 36.0 %attend.1 = bf16[8,256,128]{2,1,0:T(8,128)(2,1)} custom-call(s32[2,73]{1,0:T(2,128)} %convert_reduce_fusion.at_ref, bf16[8,768,128]{2,1,0:T(8,128)(2,1)} %all-to-all-done.1.x_ref), custom_call_target="tpu_custom_call" | custom-call | flops 20000000000 | bytes 3145728 | tf_op jit(solution)/shard_map/attend/pallas_call | solution.py:357
  152.1 0.0 all-to-all-done.2.dqkv_ref
  152.1 0.0 copy-start
  152.1 4.2 %all-to-all-start.3 = ((bf16[8,256,128]{2,1,0:T(8,128)(2,1)}), bf16[8,256,128]{2,1,0:T(8,128)(2,1)S(1)}, u32[]{:S(2)}, u32[]{:S(2)}) async-start(bf16[8,256,128]{2,1,0:T(8,128)(2,1)} %attend.1), calls=%async_computation.3 | async-start | bytes 1048576 | tf_op jit(solution)/shard_map/all_to_all | solution.py:393
  156.3 0.0 copy-done
  156.3 4.8 %input_grad.1 = bf16[512,512]{1,0:T(8,128)(2,1)} custom-call(s32[1]{0:T(128)} %copy.19.pick_ref, bf16[8,768,128]{2,1,0:T(8,128)(2,1)} %copy-done, bf16[4,512,512]{2,1,0:T(8,128)(2,1)} %bitcast.17, bf16[512,512]{1,0:T(8,128)(2,1)} %bitcast.19, f32[1,512]{1,0:T(1,128)} %gain_ref.5, bf16[512,1536]{1,0:T(8,128)(2,1)} %bitcast.15), custom_call_target="tpu_custom_call" | custom-call | flops 805306368 | bytes 5242880 | tf_op jit(solution)/shard_map/input_grad/pallas_call | solution.py:371
  161.1 4.1 %collective-permute-start.1 = (bf16[1,512,512]{2,1,0:T(8,128)(2,1)}, bf16[1,512,512]{2,1,0:T(8,128)(2,1)S(1)}, u32[]{:S(2)}, u32[]{:S(2)}) collective-permute-start(bf16[1,512,512]{2,1,0:T(8,128)(2,1)} %bitcast.24), channel_id=1, source_target_pairs={{8,0},{16,8},{24,16},{9,1},{17,9},{25,17},{10,2},{18,10},{26,18},{... | collective-permute-start | bytes 1572872 | tf_op jit(solution)/shard_map/ppermute | solution.py:31
  165.3 0.0 all-to-all-done.3.att_ref
  165.3 0.0 copy-start.2
  165.3 0.8 copy-done.2
  166.1 2.7 %mix.1 = bf16[512,512]{1,0:T(8,128)(2,1)} custom-call(bf16[8,256,128]{2,1,0:T(8,128)(2,1)} %copy-done.2, bf16[512,512]{1,0:T(8,128)(2,1)} %bitcast.23, bf16[512,512]{1,0:T(8,128)(2,1)} %bitcast.21), custom_call_target="tpu_custom_call" | custom-call | flops 268435456 | bytes 2097152 | tf_op jit(solution)/shard_map/mix/pallas_call | solution.py:357
  168.8 1.9 %collective-permute-start = (bf16[1,512,512]{2,1,0:T(8,128)(2,1)}, bf16[1,512,512]{2,1,0:T(8,128)(2,1)S(1)}, u32[]{:S(2)}, u32[]{:S(2)}) collective-permute-start(bf16[1,512,512]{2,1,0:T(8,128)(2,1)} %bitcast.25), channel_id=1, source_target_pairs={{0,8},{8,16},{16,24},{1,9},{9,17},{17,25},{2,10},{10,18},{18,26},{... | collective-permute-start | bytes 1572872 | tf_op jit(solution)/shard_map/ppermute | solution.py:31
  170.7 6.5 %collective-permute-done.1 = bf16[1,512,512]{2,1,0:T(8,128)(2,1)S(1)} collective-permute-done((bf16[1,512,512]{2,1,0:T(8,128)(2,1)}, bf16[1,512,512]{2,1,0:T(8,128)(2,1)S(1)}, u32[]{:S(2)}, u32[]{:S(2)}) %collective-permute-start.1) | collective-permute-done | bytes 524320 | tf_op jit(solution)/shard_map/ppermute | solution.py:31
  177.2 7.4 %collective-permute-done = bf16[1,512,512]{2,1,0:T(8,128)(2,1)S(1)} collective-permute-done((bf16[1,512,512]{2,1,0:T(8,128)(2,1)}, bf16[1,512,512]{2,1,0:T(8,128)(2,1)S(1)}, u32[]{:S(2)}, u32[]{:S(2)}) %collective-permute-start) | collective-permute-done | bytes 524320 | tf_op jit(solution)/shard_map/ppermute | solution.py:31
  184.6 0.8 copy.20
  185.4 0.8 copy.21
  (5 shorter events, 0.0 us)
Async XLA Ops:
  8.8 29.7 %all-to-all-start = ((bf16[8,1040,128]{2,1,0:T(8,128)(2,1)}), bf16[8,1040,128]{2,1,0:T(8,128)(2,1)S(1)}, u32[]{:S(2)}, u32[]{:S(2)}) async-start(bf16[8,1040,128]{2,1,0:T(8,128)(2,1)} %project_grad.1), calls=%async_computation | async-start | bytes 4259840 | tf_op jit(solution)/shard_map/all_to_all | solution.py:393
  38.5 5.7 %copy-start.1 = (bf16[8,1040,128]{2,1,0:T(8,128)(2,1)}, bf16[8,1040,128]{2,1,0:T(8,128)(2,1)S(1)}, u32[]{:S(2)}) copy-start(bf16[8,1040,128]{2,1,0:T(8,128)(2,1)S(1)} %all-to-all-done.x_ref) | copy-start | bytes 6389764
  38.5 73.4 %all-to-all-start.1 = ((bf16[8,768,128]{2,1,0:T(8,128)(2,1)}), bf16[8,768,128]{2,1,0:T(8,128)(2,1)}, u32[]{:S(2)}, u32[]{:S(2)}) async-start(bf16[8,768,128]{2,1,0:T(8,128)(2,1)} %project.1), calls=%async_computation.1 | async-start | bytes 3145728 | tf_op jit(solution)/shard_map/all_to_all | solution.py:393
  111.9 40.2 %all-to-all-start.2 = ((bf16[8,768,128]{2,1,0:T(8,128)(2,1)}), bf16[8,768,128]{2,1,0:T(8,128)(2,1)S(1)}, u32[]{:S(2)}, u32[]{:S(2)}) async-start(bf16[8,768,128]{2,1,0:T(8,128)(2,1)} %attend_grad.1), calls=%async_computation.2 | async-start | bytes 3145728 | tf_op jit(solution)/shard_map/all_to_all | solution.py:393
  152.1 4.2 %copy-start = (bf16[8,768,128]{2,1,0:T(8,128)(2,1)}, bf16[8,768,128]{2,1,0:T(8,128)(2,1)S(1)}, u32[]{:S(2)}) copy-start(bf16[8,768,128]{2,1,0:T(8,128)(2,1)S(1)} %all-to-all-done.2.dqkv_ref) | copy-start | bytes 4718596
  152.1 13.1 %all-to-all-start.3 = ((bf16[8,256,128]{2,1,0:T(8,128)(2,1)}), bf16[8,256,128]{2,1,0:T(8,128)(2,1)S(1)}, u32[]{:S(2)}, u32[]{:S(2)}) async-start(bf16[8,256,128]{2,1,0:T(8,128)(2,1)} %attend.1), calls=%async_computation.3 | async-start | bytes 1048576 | tf_op jit(solution)/shard_map/all_to_all | solution.py:393
  161.1 16.1 %collective-permute-start.1 = (bf16[1,512,512]{2,1,0:T(8,128)(2,1)}, bf16[1,512,512]{2,1,0:T(8,128)(2,1)S(1)}, u32[]{:S(2)}, u32[]{:S(2)}) collective-permute-start(bf16[1,512,512]{2,1,0:T(8,128)(2,1)} %bitcast.24), channel_id=1, source_target_pairs={{8,0},{16,8},{24,16},{9,1},{17,9},{25,17},{10,2},{18,10},{26,18},{... | collective-permute-start | bytes 1572872 | tf_op jit(solution)/shard_map/ppermute | solution.py:31
  165.3 0.8 copy-start.2
  168.8 15.8 %collective-permute-start = (bf16[1,512,512]{2,1,0:T(8,128)(2,1)}, bf16[1,512,512]{2,1,0:T(8,128)(2,1)S(1)}, u32[]{:S(2)}, u32[]{:S(2)}) collective-permute-start(bf16[1,512,512]{2,1,0:T(8,128)(2,1)} %bitcast.25), channel_id=1, source_target_pairs={{0,8},{8,16},{16,24},{1,9},{9,17},{17,25},{2,10},{10,18},{18,26},{... | collective-permute-start | bytes 1572872 | tf_op jit(solution)/shard_map/ppermute | solution.py:31
